TPU v7x, 512 devices: a whole 4x8x8 slice. The times are simulated.
512 devices in a mesh: req: 64 (over x, z, core), wt: 8 (over y).
Axes of the slice: x: 4, y: 8, z: 8, core: 2. Of those that a mesh axis runs over, the one named last changes fastest.
Arguments:
- streams: bfloat16 [4, 32768, 2048], P(None, 'req', 'wt'), may hold values from -6 to 6
- doc_ids: int32 [64, 512], P('req'), may hold values from 0 to 3, never falling along the last dimension, each value on 1 to 256 neighbouring positions
- doc_adapter: int32 [64, 4, 1], P('req'), may hold values from 0 to 15
- width_weights: float32 [4], replicated, may hold values from 0.2 to 1
- stream_mixing: float32 [4, 4], replicated, may hold values from -3 to 3
- depth_static: float32 [4], replicated, may hold values from 0.2 to 1
- depth_dir: bfloat16 [2048, 4], replicated, may hold values from -0.125 to 0.125
- qkv_weight: bfloat16 [2048, 3, 2048], P('req', None, 'wt')
- adapter_down: bfloat16 [16, 2048, 16], P('wt'), may hold values from -0.125 to 0.125
- adapter_up: bfloat16 [16, 16, 3, 2048], P(None, None, None, 'wt'), may hold values from -1.5 to 1.5
- out_weight: bfloat16 [2048, 2048], P('req', 'wt'), may hold values from -0.125 to 0.125
- page_slot: int32 [2048], P('req'), may hold values from 0 to 2047, as said below
Outputs:
- new_streams: bfloat16 [4, 32768, 2048], P(None, 'req', 'wt')
- kv_pool: bfloat16 [2048, 16, 2, 2048], P('req', None, None, 'wt')
Inputs may be any that keep to these rules, and one draw needn't show every extreme that they name: page_slot is a permutation of all page slots; page p lands on index page_slot[p] // 32 of req; the pages 2k and 2k + 1 form one request and land on the same index; of the pages of one index of req at most 2 land on any one index, and exactly 2 on some.
All inputs are finite; a program needn't handle non-finite values.
Results may differ from a plain program's by a relative error of at most 0.008.
Values may be sent and summed in bfloat16 or wider, within the bound.
A program may use at most 64 MiB of HBM per device.

v0:
```python
import math

import jax
import jax.numpy as jnp
from jax import lax
from jax.sharding import PartitionSpec as P

HD = 128
R = 16
PAGE = 16


EPSILON = 1e-05


def body(
    streams,
    doc_ids,
    doc_adapter,
    width_weights,
    stream_mixing,
    depth_static,
    depth_dir,
    qkv_weight,
    adapter_down,
    adapter_up,
    out_weight,
    page_slot,
):
    count_streams = streams.shape[0]
    tokens = streams.shape[1]
    mixed_local = width_weights[0] * streams[0].astype(jnp.float32)
    for stream in range(1, count_streams):
        mixed_local = mixed_local + width_weights[stream] * streams[stream].astype(jnp.float32)
    gathered = lax.all_gather(mixed_local.astype(jnp.bfloat16), "wt", axis=1, tiled=True)
    widened = gathered.astype(jnp.float32)
    normed = (
        widened * lax.rsqrt(jnp.mean(widened * widened, axis=-1, keepdims=True) + EPSILON)
    ).astype(jnp.bfloat16)
    segment = doc_ids[0]
    doc_table = doc_adapter[0, :, 0]
    token_adapter = jnp.sum(
        jnp.where(
            segment[:, None] == jnp.arange(doc_table.shape[0])[None, :], doc_table[None, :], 0
        ),
        axis=1,
    )
    adapters_total = adapter_up.shape[0]
    selector = (token_adapter[:, None] == jnp.arange(adapters_total)[None, :]).astype(jnp.float32)
    every_rank = jnp.einsum(
        "td,adr->tar",
        normed,
        lax.all_gather(adapter_down, "wt", axis=0, tiled=True),
        preferred_element_type=jnp.float32,
    )
    shrunk = jnp.sum(selector[:, :, None] * every_rank, axis=1)
    shrunk = shrunk.astype(jnp.bfloat16)
    spread = (
        (selector[:, :, None] * shrunk.astype(jnp.float32)[:, None, :])
        .reshape(tokens, adapters_total * R)
        .astype(jnp.bfloat16)
    )
    lowrank = jnp.dot(
        spread, adapter_up.reshape(adapters_total * R, -1), preferred_element_type=jnp.float32
    )
    width_local = qkv_weight.shape[2]
    portion = lax.all_gather(qkv_weight, "req", axis=0, tiled=True)
    base = jnp.dot(
        normed, portion.reshape(portion.shape[0], -1), preferred_element_type=jnp.float32
    )
    heads_local = width_local // HD
    projected = (base + lowrank).astype(jnp.bfloat16).reshape(tokens, 3, heads_local, HD)
    key_rows = projected[:, 1]
    value_rows = projected[:, 2]
    block_rows = min(512, tokens)
    blocks = tokens // block_rows
    positions = jnp.arange(tokens)

    def attend(packed):
        query_block, query_pos, query_seg = packed
        scores = jnp.einsum(
            "qhd,khd->hqk", query_block, key_rows, preferred_element_type=jnp.float32
        ) / math.sqrt(HD)
        allowed = (query_seg[:, None] == segment[None, :]) & (
            positions[None, :] <= query_pos[:, None]
        )
        scores = jnp.where(allowed[None], scores, -1e30)
        highest = jnp.max(scores, axis=-1, keepdims=True)
        weights = jnp.exp(scores - highest)
        weights = (weights / jnp.sum(weights, axis=-1, keepdims=True)).astype(jnp.bfloat16)
        return jnp.einsum(
            "hqk,khd->qhd", weights, value_rows, preferred_element_type=jnp.float32
        ).astype(jnp.bfloat16)

    attended = lax.map(
        attend,
        (
            projected[:, 0].reshape(blocks, block_rows, heads_local, HD),
            positions.reshape(blocks, block_rows),
            segment.reshape(blocks, block_rows),
        ),
    )
    attended = attended.reshape(tokens, width_local)
    every_row = lax.all_gather(out_weight, "req", axis=0, tiled=True)
    own_rows = lax.all_to_all(every_row, "wt", split_axis=0, concat_axis=1, tiled=True)
    layer_out = lax.psum_scatter(
        jnp.dot(attended, own_rows, preferred_element_type=jnp.float32).astype(jnp.bfloat16),
        "wt",
        scatter_dimension=1,
        tiled=True,
    ).astype(jnp.float32)
    depth = depth_static[None, :] + jnp.tanh(
        jnp.dot(normed, depth_dir, preferred_element_type=jnp.float32)
    )
    outputs = []
    for stream in range(count_streams):
        carried = stream_mixing[stream, 0] * streams[0].astype(jnp.float32)
        for source in range(1, count_streams):
            carried = carried + stream_mixing[stream, source] * streams[source].astype(jnp.float32)
        outputs.append((carried + depth[:, stream][:, None] * layer_out).astype(jnp.bfloat16))
    new_streams = jnp.stack(outputs)
    page_count = page_slot.shape[0]
    cache = projected[:, 1:3].reshape(page_count, PAGE, 2, width_local)
    groups = lax.axis_size("req")
    capacity = 2 * max(1, page_count // (2 * groups))
    target_dev = page_slot // page_count
    local_slot = page_slot % page_count
    ordinal = jnp.arange(page_count)
    earlier = (target_dev[None, :] == target_dev[:, None]) & (ordinal[None, :] < ordinal[:, None])
    placement = target_dev * capacity + jnp.sum(earlier.astype(jnp.int32), axis=1)
    outgoing = (
        jnp.zeros((groups * capacity, PAGE, 2, width_local), jnp.bfloat16).at[placement].set(cache)
    )
    labels = (
        jnp.full((groups * capacity,), -1.0, jnp.bfloat16)
        .at[placement]
        .set(local_slot.astype(jnp.bfloat16))
    )
    incoming, arrived = (
        lax.all_to_all(outgoing, "req", split_axis=0, concat_axis=0, tiled=True),
        lax.all_to_all(labels, "req", split_axis=0, concat_axis=0, tiled=True),
    )
    slot_index = arrived.astype(jnp.int32)
    slot_index = jnp.where(slot_index < 0, page_count, slot_index)
    kv_pool = (
        jnp.zeros((page_count + 1, PAGE, 2, width_local), jnp.bfloat16)
        .at[slot_index]
        .set(incoming)[:page_count]
    )
    return (new_streams, kv_pool)


def solution(mesh):
    in_specs = (
        P(None, "req", "wt"),
        P("req", None),
        P("req", None, None),
        P(),
        P(),
        P(),
        P(),
        P("req", None, "wt"),
        P("wt", None, None),
        P(None, None, None, "wt"),
        P("req", "wt"),
        P("req"),
    )
    out_specs = (P(None, "req", "wt"), P("req", None, None, "wt"))
    return jax.shard_map(body, mesh=mesh, in_specs=in_specs, out_specs=out_specs, check_vma=False)
```

profile of v0, /device:TPU:1, one launch (start us, length us, event | category | flops | bytes accessed | tf_op | source)
XLA Modules:
  0.0 408.4 jit_solution(16914693759775817778)
XLA Ops:
  7.2 0.7 all-gather.10.cloned.1.call-update
  8.0 1.5 fusion.59
  9.4 4.6 %fusion.24 = bf16[1,512,256]{2,1,0:T(8,128)(2,1)} fusion(f32[]{:T(128)} %bitcast.8, f32[]{:T(128)} %bitcast.7, f32[]{:T(128)} %bitcast.6, f32[]{:T(128)} %bitcast.5, bf16[4,512,256]{2,1,0:T(8,128)(2,1)} %param.12), kind=kLoop, calls=%fused_computation.62 | loop fusion | flops 1572864 | bytes 1310736 | tf_op jit(solution)/shard_map/convert_element_type | solution.py:35
  15.4 84.8 %all-gather.10.cloned.1.call-done = bf16[2048,256]{1,0:T(8,128)(2,1)} async-done(((bf16[32,256]{1,0:T(8,128)(2,1)}), bf16[2048,256]{1,0:T(8,128)(2,1)}) %all-gather.10.cloned.1.call-update) | async-done | bytes 1048592 | tf_op jit(solution)/shard_map/all_gather | solution.py:104
  100.2 6.5 %all-to-all-start = ((bf16[8,256,256]{2,1,0:T(8,128)(2,1)}), bf16[8,256,256]{2,1,0:T(8,128)(2,1)S(1)}, u32[]{:S(2)}, u32[]{:S(2)}) async-start(bf16[8,256,256]{2,1,0:T(8,128)(2,1)} %bitcast.120), calls=%async_computation | async-start | bytes 2097152 | tf_op jit(solution)/shard_map/all_to_all | solution.py:105
  107.6 0.7 convert_reduce_fusion.1
  109.0 0.9 fusion.7
  109.9 50.0 %all-gather.12.cloned.1.call-done = bf16[1,512,2048]{2,1,0:T(8,128)(2,1)} async-done(((bf16[1,512,256]{2,1,0:T(8,128)(2,1)}), bf16[1,512,2048]{2,1,0:T(8,128)(2,1)}) %all-gather.12.cloned.1.call-update) | async-done | bytes 2097168 | tf_op jit(solution)/shard_map/all_gather | solution.py:35
  159.9 2.2 fusion.1
  162.8 34.9 %all-gather.8.cloned.1.call-done = bf16[16,2048,16]{1,2,0:T(8,128)(2,1)} async-done(((bf16[2,2048,16]{1,2,0:T(8,128)(2,1)}), bf16[16,2048,16]{1,2,0:T(8,128)(2,1)}) %all-gather.8.cloned.1.call-update) | async-done | bytes 1048592 | tf_op jit(solution)/shard_map/all_gather | solution.py:53
  197.7 2.1 fusion.51
  200.4 88.9 %all-gather.6.cloned.1.call-done = bf16[2048,3,256]{2,0,1:T(8,128)(2,1)} async-done(((bf16[32,3,256]{2,0,1:T(8,128)(2,1)}), bf16[2048,3,256]{2,0,1:T(8,128)(2,1)}) %all-gather.6.cloned.1.call-update) | async-done | bytes 3145744 | tf_op jit(solution)/shard_map/all_gather | solution.py:67
  289.4 4.7 %copy.49 = bf16[2048,3,256]{0,2,1:T(8,128)(2,1)} copy(bf16[2048,3,256]{2,0,1:T(8,128)(2,1)} %all-gather.6.cloned.1.call-done) | data formatting | bytes 6291456 | tf_op jit(solution)/shard_map/all_gather | solution.py:67
  294.1 4.4 %fusion.53 = f32[512,768]{1,0:T(8,128)S(1)} fusion(bf16[2048,768]{0,1:T(8,128)(2,1)} %bitcast.116, bf16[1,512,2048]{2,1,0:T(8,128)(2,1)} %all-gather.12.cloned.1.call-done, f32[512]{0:T(512)S(1)} %copy-done.9), kind=kOutput, calls=%fused_computation.110 | convolution fusion | flops 1613758464 | bytes 6817792 | tf_op jit(solution)/shard_map/dot_general | solution.py:68
  299.9 2.3 fusion.60
  302.1 1.9 convolution_convert_fusion.1
  304.1 2.1 convolution_convert_fusion
  306.2 0.9 scatter_custom_fusion
  307.1 0.8 all_to_all.30
  307.9 6.3 %all-to-all-start.1 = ((bf16[64,2,1]{1,2,0:T(2,128)(2,1)}), bf16[64,2,1]{1,2,0:T(2,128)(2,1)S(1)}, u32[]{:S(2)}, u32[]{:S(2)}) async-start(bf16[64,2,1]{1,2,0:T(2,128)(2,1)} %all_to_all.30), calls=%async_computation.2 | async-start | bytes 65536 | tf_op jit(solution)/shard_map/all_to_all | solution.py:141
  315.0 1.6 broadcast_in_dim.85
  316.6 4.3 %scatter_fusion = bf16[128,16,2,256]{3,1,2,0:T(8,128)(2,1)} fusion(bf16[128,16,2,256]{3,1,2,0:T(8,128)(2,1)} %broadcast_in_dim.85, s32[32]{0:T(128)S(1)} %compare_select_fusion.2, bf16[32,16,2,256]{3,1,2,0:T(8,128)(2,1)S(1)} %copy.58), kind=kCustom, calls=%fused_computation.1 | custom fusion | bytes 1572992 | tf_op jit(solution)/shard_map/scatter | solution.py:132
  321.0 2.5 all-to-all-done.1
  323.5 8.0 %all-to-all-start.2 = ((bf16[128,16,2,256]{3,1,2,0:T(8,128)(2,1)}), bf16[128,16,2,256]{3,1,2,0:T(8,128)(2,1)S(1)}, u32[]{:S(2)}, u32[]{:S(2)}) async-start(bf16[128,16,2,256]{3,1,2,0:T(8,128)(2,1)} %scatter_fusion), calls=%async_computation.3 | async-start | bytes 4194304 | tf_op jit(solution)/shard_map/all_to_all | solution.py:140
  331.5 0.7 fusion.58
  332.5 2.3 fusion.4
  334.9 47.8 %all-to-all-done.2 = bf16[128,16,2,256]{3,1,2,0:T(8,128)(2,1)S(1)} async-done(((bf16[128,16,2,256]{3,1,2,0:T(8,128)(2,1)}), bf16[128,16,2,256]{3,1,2,0:T(8,128)(2,1)S(1)}, u32[]{:S(2)}, u32[]{:S(2)}) %all-to-all-start.2) | async-done | bytes 2097184 | tf_op jit(solution)/shard_map/all_to_all | solution.py:140
  382.8 4.6 %scatter_fusion.1 = bf16[33,16,2,256]{3,1,2,0:T(8,128)(2,1)S(1)} fusion(bf16[33,16,2,256]{3,1,2,0:T(8,128)(2,1)S(1)} %broadcast_in_dim.81, s32[128]{0:T(128)S(1)} %fusion.46, bf16[128,16,2,256]{3,1,2,0:T(8,128)(2,1)S(1)} %all-to-all-done.2), kind=kCustom, calls=%fused_computation.2 | custom fusion | bytes 6291968 | tf_op jit(solution)/shard_map/scatter | solution.py:148
  387.5 1.3 copy.59
  388.8 6.4 %fusion.40 = (bf16[1,512,256]{2,1,0:T(8,128)(2,1)S(1)}, bf16[1,512,256]{2,1,0:T(8,128)(2,1)S(1)}) fusion(bf16[512,256]{1,0:T(8,128)(2,1)} %reduce-scatter.2.cloned.1.call-done, f32[512]{0:T(512)S(1)} %bitcast.128, f32[]{:T(128)} %bitcast.38, f32[]{:T(128)} %bitcast.37, f32[]{:T(128)} %bitcast.36, f32[]{:T(128)} %bitcast.35, ...), kind=kLoop, calls=%fused_computation.82 | loop fusion | flops 3276800 | bytes 1839136 | tf_op jit(solution)/shard_map/stack | solution.py:121
  395.2 5.5 %fusion.42 = (bf16[1,512,256]{2,1,0:T(8,128)(2,1)S(1)}, bf16[1,512,256]{2,1,0:T(8,128)(2,1)S(1)}) fusion(bf16[512,256]{1,0:T(8,128)(2,1)S(1)} %copy-done.3, f32[512]{0:T(512)S(1)} %bitcast.125, f32[]{:T(128)} %bitcast.3, f32[]{:T(128)} %bitcast.2, f32[]{:T(128)} %bitcast.1, f32[]{:T(128)} %bitcast, bf16[4,512,256]{2,1,0:T(8,128)(2,1)S(1)} %copy-done.1, ...), kind=kLoop, calls=%fused_computation.84 | loop fusion | flops 3276800 | bytes 1839136 | tf_op jit(solution)/shard_map/stack | solution.py:121
  400.7 1.1 pad_maximum_fusion
  (69 shorter events, 6.8 us)
Async XLA Ops:
  7.2 325.3 %copy-start = (bf16[2048,4]{0,1:T(4,128)(2,1)S(1)}, bf16[2048,4]{0,1:T(4,128)(2,1)}, u32[]{:S(2)}) copy-start(bf16[2048,4]{0,1:T(4,128)(2,1)} %param.18) | copy-start | bytes 49156
  7.2 99.5 %copy-start.12 = (s32[32]{0:T(128)S(1)}, s32[32]{0:T(128)}, u32[]{:S(2)}) copy-start(s32[32]{0:T(128)} %param.23) | copy-start | bytes 388
  7.2 100.0 %copy-start.4 = (bf16[16,16,3,256]{3,1,2,0:T(8,128)(2,1)S(1)}, bf16[16,16,3,256]{3,1,2,0:T(8,128)(2,1)}, u32[]{:S(2)}) copy-start(bf16[16,16,3,256]{3,1,2,0:T(8,128)(2,1)} %param.21) | copy-start | bytes 1179652
  7.2 93.0 %all-gather.10.cloned.1.call-start = ((), (), s32[]{:S(2)}) async-start(), calls=%async_computation.6 | async-start | bytes 1064960 | tf_op jit(solution)/shard_map/all_gather | solution.py:104
  7.9 152.0 %all-gather.12.cloned.1.call-start = ((), (), s32[]{:S(2)}) async-start(), calls=%async_computation.8 | async-start | bytes 2359296 | tf_op jit(solution)/shard_map/all_gather | solution.py:35
  14.1 94.2 %copy-start.8 = (s32[1,512]{1,0:T(1,128)S(1)}, s32[1,512]{1,0:T(1,128)}, u32[]{:S(2)}) copy-start(s32[1,512]{1,0:T(1,128)} %param.13) | copy-start | bytes 6148
  14.1 94.2 %copy-start.11 = (s32[1,4,1]{1,2,0:T(1,128)S(1)}, s32[1,4,1]{1,2,0:T(1,128)}, u32[]{:S(2)}) copy-start(s32[1,4,1]{1,2,0:T(1,128)} %param.14) | copy-start | bytes 52
  14.1 183.6 %all-gather.8.cloned.1.call-start = ((), (), s32[]{:S(2)}) async-start(), calls=%async_computation.5 | async-start | bytes 1179648 | tf_op jit(solution)/shard_map/all_gather | solution.py:53
  14.8 274.5 %all-gather.6.cloned.1.call-start = ((), (), s32[]{:S(2)}) async-start(), calls=%async_computation.4 | async-start | bytes 3194880 | tf_op jit(solution)/shard_map/all_gather | solution.py:67
  100.2 99.7 %all-to-all-start = ((bf16[8,256,256]{2,1,0:T(8,128)(2,1)}), bf16[8,256,256]{2,1,0:T(8,128)(2,1)S(1)}, u32[]{:S(2)}, u32[]{:S(2)}) async-start(bf16[8,256,256]{2,1,0:T(8,128)(2,1)} %bitcast.120), calls=%async_computation | async-start | bytes 2097152 | tf_op jit(solution)/shard_map/all_to_all | solution.py:105
  106.7 282.1 %reduce-scatter.2.cloned.1.call-start = ((), (), s32[]{:S(2)}) async-start(), calls=%async_computation.7 | async-start | bytes 2359296 | tf_op jit(solution)/shard_map/reduce_scatter | solution.py:106
  107.2 1.8 copy-start.14
  159.9 37.7 %copy-start.2 = (bf16[1,512,2048]{2,1,0:T(8,128)(2,1)S(1)}, bf16[1,512,2048]{2,1,0:T(8,128)(2,1)}, u32[]{:S(2)}) copy-start(bf16[1,512,2048]{2,1,0:T(8,128)(2,1)} %all-gather.12.cloned.1.call-done) | copy-start | bytes 6291460
  197.7 2.1 copy-start.5
  200.4 93.7 %copy-start.9 = (f32[512]{0:T(512)S(1)}, f32[512]{0:T(512)}, u32[]{:S(2)}) copy-start(f32[512]{0:T(512)} %add_rsqrt_fusion) | copy-start | bytes 6148
  298.9 1.0 copy-start.6
  304.0 2.1 copy-start.15
  304.1 2.1 copy-start.16
  307.9 15.6 %all-to-all-start.1 = ((bf16[64,2,1]{1,2,0:T(2,128)(2,1)}), bf16[64,2,1]{1,2,0:T(2,128)(2,1)S(1)}, u32[]{:S(2)}, u32[]{:S(2)}) async-start(bf16[64,2,1]{1,2,0:T(2,128)(2,1)} %all_to_all.30), calls=%async_computation.2 | async-start | bytes 65536 | tf_op jit(solution)/shard_map/all_to_all | solution.py:141
  321.0 10.5 %copy-start.7 = (f32[4,4]{1,0:T(4,128)S(1)}, f32[4,4]{1,0:T(4,128)}, u32[]{:S(2)}) copy-start(f32[4,4]{1,0:T(4,128)} %param.16) | copy-start | bytes 196
  321.0 11.5 %copy-start.10 = (f32[512]{0:T(512)S(1)}, f32[512]{0:T(512)}, u32[]{:S(2)}) copy-start(f32[512]{0:T(512)} %add_rsqrt_fusion) | copy-start | bytes 6148
  321.0 11.5 %copy-start.13 = (f32[4]{0:T(128)S(1)}, f32[4]{0:T(128)}, u32[]{:S(2)}) copy-start(f32[4]{0:T(128)} %param.17) | copy-start | bytes 52
  323.5 59.2 %all-to-all-start.2 = ((bf16[128,16,2,256]{3,1,2,0:T(8,128)(2,1)}), bf16[128,16,2,256]{3,1,2,0:T(8,128)(2,1)S(1)}, u32[]{:S(2)}, u32[]{:S(2)}) async-start(bf16[128,16,2,256]{3,1,2,0:T(8,128)(2,1)} %scatter_fusion), calls=%async_computation.3 | async-start | bytes 4194304 | tf_op jit(solution)/shard_map/all_to_all | solution.py:140
  387.4 1.4 copy-start.1
  388.8 6.4 %copy-start.3 = (bf16[512,256]{1,0:T(8,128)(2,1)S(1)}, bf16[512,256]{1,0:T(8,128)(2,1)}, u32[]{:S(2)}) copy-start(bf16[512,256]{1,0:T(8,128)(2,1)} %reduce-scatter.2.cloned.1.call-done) | copy-start | bytes 786436
Sparse Core Ops, SparseCore 0:
  11.4 88.7 all-gather.9
  102.8 57.1 all-gather.11
  162.0 35.5 all-gather.7
  200.9 88.4 all-gather.5
  306.3 37.3 reduce-scatter.1
where the time goes:
time: 409 us; the launch traced here: 408 us
  waiting for transfers between devices  311 us (76%)
  other arithmetic  23.5 us (6%)
  local copies, waits for them, and re-layouts  23.4 us (6%)
  starting transfers between devices  21 us (5%)
  matrix products  15.4 us (4%)
  between operations  14.1 us (3%)
    all_gather x1, waiting for transfers between devices, body(): portion = lax.all_gather(qkv_weight, 'req', axis=0, tiled=True)  88.9 us
    all_gather x1, waiting for transfers between devices, body(): every_row = lax.all_gather(out_weight, 'req', axis=0, tiled=True)  84.8 us
    all_gather x1, waiting for transfers between devices, body(): lax.all_gather(mixed_local.astype(jnp.bfloat16), 'wt', axis=1, tiled=True)  50 us
    all_to_all x1, waiting for transfers between devices, body(): lax.all_to_all(outgoing, 'req', split_axis=0, concat_axis=0, tiled=True)  47.8 us
    all_gather x1, waiting for transfers between devices, body(): lax.all_gather(adapter_down, 'wt', axis=0, tiled=True)  34.9 us
    another operation x3, other arithmetic, body(): new_streams = jnp.stack(outputs)  13 us
  transfers between devices with their start and end apart: 8, of which 6 were waited for; matrix products, arithmetic and copies ran while one was open for 8% of the time, Pallas kernels for 0%

commit v1 on v0

v1 whole, which is shorter than its diff:
```python
import functools
import math

import jax
import jax.numpy as jnp
from jax import lax
from jax.experimental import pallas as pl
from jax.experimental.pallas import tpu as pltpu
from jax.sharding import PartitionSpec as P

HD = 128
R = 16
PAGE = 16
NX, NZ, NC, NY = 4, 8, 2, 8

EPSILON = 1e-05
MESH = pl.DeviceIdType.MESH


class Copies:
    def __init__(self, send_sem, recv_sem):
        self.send_sem, self.recv_sem = send_sem, recv_sem
        self.count = 0
        self.started = []

    def start(self, src, dst, req, wt):
        index = self.count
        self.count += 1
        copy = pltpu.make_async_remote_copy(
            src_ref=src,
            dst_ref=dst,
            send_sem=self.send_sem.at[index],
            recv_sem=self.recv_sem.at[index],
            device_id=(req, wt),
            device_id_type=MESH,
        )
        copy.start()
        self.started.append(copy)
        return copy

    def finish(self):
        for copy in self.started:
            copy.wait_send()


def position():
    req = lax.axis_index("req")
    wt = lax.axis_index("wt")
    core = lax.rem(req, NC)
    z = lax.rem(req // NC, NZ)
    x = req // (NC * NZ)
    return req, wt, x, z, core


def turn(value, shift, size):
    return lax.rem(value + (shift + size), size)


def meet(partners):
    barrier = pltpu.get_barrier_semaphore()
    for req, wt in partners:
        pl.semaphore_signal(barrier, inc=1, device_id=(req, wt), device_id_type=MESH)
    pl.semaphore_wait(barrier, len(partners))


def columns(ref, half, origin):
    rows = ref.shape[0] // 2
    width = ref.shape[1] // NY
    return ref.at[pl.ds(half * rows, rows), pl.ds(pl.multiple_of(origin * width, width), width)]


def token_hop(copies, held, own, out, req, wt, half, direction, step):
    if step == 3 and half != (0 if direction == 1 else 1):
        return
    key = (half, direction)
    if step > 0:
        held[key].wait_recv()
    origin = turn(wt, -direction * step, NY)
    rows = out.shape[0] // 2
    src = own.at[pl.ds(half * rows, rows)] if step == 0 else columns(out, half, origin)
    held[key] = copies.start(src, columns(out, half, origin), req, turn(wt, direction, NY))


def gather_kernel(mixed, rows, down, mixed_all, rows_all, down_all, send_sem, recv_sem, local_sem):
    req, wt, x, z, core = position()
    partner = req + 1 - 2 * core

    def at(x_at, z_at):
        return (x_at * NZ + z_at) * NC + core

    def near_x(shift):
        return at(turn(x, shift, NX), z)

    def near_z(shift):
        return at(x, turn(z, shift, NZ))

    meet(
        [(req, turn(wt, 1, NY)), (req, turn(wt, -1, NY)), (partner, wt)]
        + [(near_x(1), wt), (near_x(-1), wt), (near_z(1), wt), (near_z(-1), wt)]
    )
    copies = Copies(send_sem, recv_sem)
    held_tokens, held_down, held_rows = {}, {}, {}

    def rows_hop(unit, direction, step):
        if step == 3 and unit % 2 != (0 if direction == 1 else 1):
            return
        key = (unit, direction)
        if step > 0:
            held_rows[key].wait_recv()
        block = rows_all.at[turn(x, -unit, NX), turn(z, -direction * step, NZ), core]
        src = rows if (step == 0 and unit == 0) else block
        held_rows[key] = copies.start(src, block, near_z(direction), wt)

    def down_hop(direction, step):
        if step == 3 and direction == -1:
            return
        if step > 0:
            held_down[direction].wait_recv()
        block = down_all.at[turn(wt, -direction * step, NY), core]
        src = down.at[core] if step == 0 else block
        held_down[direction] = copies.start(src, block, req, turn(wt, direction, NY))

    def share(z_shift):
        block = rows_all.at[:, turn(z, z_shift, NZ), core]
        return copies.start(block, block, partner, wt)

    own_rows = rows_all.at[x, z, core]
    from_left = copies.start(rows, own_rows, near_x(1), wt)
    from_right = copies.start(rows, own_rows, near_x(-1), wt)
    for direction in (1, -1):
        token_hop(copies, held_tokens, mixed, mixed_all, req, wt, 0, direction, 0)
        rows_hop(0, direction, 0)
    for direction in (1, -1):
        token_hop(copies, held_tokens, mixed, mixed_all, req, wt, 1, direction, 0)
        down_hop(direction, 0)
    locals_ = [
        pltpu.make_async_copy(rows, own_rows, local_sem.at[0]),
        pltpu.make_async_copy(mixed.at[pl.ds(0, mixed.shape[0] // 2)], columns(mixed_all, 0, wt), local_sem.at[1]),
        pltpu.make_async_copy(
            mixed.at[pl.ds(mixed.shape[0] // 2, mixed.shape[0] // 2)], columns(mixed_all, 1, wt), local_sem.at[2]
        ),
        pltpu.make_async_copy(down.at[core], down_all.at[wt, core], local_sem.at[3]),
    ]
    for copy in locals_:
        copy.start()
    from_left.wait_recv()
    left_block = rows_all.at[turn(x, -1, NX), z, core]
    far = copies.start(left_block, left_block, near_x(1), wt)
    for direction in (1, -1):
        rows_hop(1, direction, 0)
    from_right.wait_recv()
    for direction in (1, -1):
        rows_hop(3, direction, 0)
    far.wait_recv()
    for direction in (1, -1):
        rows_hop(2, direction, 0)
    for copy in locals_:
        copy.wait()
    shared = [share(0)]
    for step in range(1, 4):
        for unit in (0, 1, 3, 2):
            for direction in (1, -1):
                rows_hop(unit, direction, step)
            if unit == 1 or unit == 2:
                for direction in (1, -1):
                    token_hop(
                        copies, held_tokens, mixed, mixed_all, req, wt, 0 if unit == 1 else 1, direction, step
                    )
        if step == 3:
            for unit in (1, 3):
                held_rows[(unit, 1)].wait_recv()
            for unit in (0, 2):
                held_rows[(unit, -1)].wait_recv()
        for direction in (1, -1):
            down_hop(direction, step)
        shared += [share(-step), share(step)]
    held_down[-1].wait_recv()
    held_down[1].wait_recv()
    every_down = down_all.at[:, core]
    shared.append(copies.start(every_down, every_down, partner, wt))
    for unit in (0, 2):
        held_rows[(unit, 1)].wait_recv()
    for unit in (1, 3):
        held_rows[(unit, -1)].wait_recv()
    shared.append(share(4))
    for half in (0, 1):
        for direction in (1, -1):
            held_tokens[(half, direction)].wait_recv()
    for copy in shared:
        copy.wait_recv()
    copies.finish()


def tokens_kernel(own, out, send_sem, recv_sem, local_sem):
    req, wt, _, _, _ = position()
    meet([(req, turn(wt, 1, NY)), (req, turn(wt, -1, NY))])
    copies = Copies(send_sem, recv_sem)
    held = {}
    rows = own.shape[0] // 2
    locals_ = []
    for step in range(4):
        for half in (0, 1):
            for direction in (1, -1):
                token_hop(copies, held, own, out, req, wt, half, direction, step)
            if step == 0:
                locals_.append(
                    pltpu.make_async_copy(own.at[pl.ds(half * rows, rows)], columns(out, half, wt), local_sem.at[half])
                )
                locals_[-1].start()
    for half in (0, 1):
        for direction in (1, -1):
            held[(half, direction)].wait_recv()
    for copy in locals_:
        copy.wait()
    copies.finish()


def spec(space):
    return pl.BlockSpec(memory_space=space)


def gather_all(mixed, rows, down):
    tokens, width = mixed.shape
    count = 3 + 28 + 8 + 14 + 7 + 1
    return pl.pallas_call(
        gather_kernel,
        out_shape=[
            jax.ShapeDtypeStruct((tokens, width * NY), mixed.dtype),
            jax.ShapeDtypeStruct((NX, NZ, NC) + rows.shape, rows.dtype),
            jax.ShapeDtypeStruct((NY,) + down.shape, down.dtype),
        ],
        in_specs=[spec(pltpu.VMEM)] * 3,
        out_specs=[spec(pl.ANY)] * 3,
        scratch_shapes=[
            pltpu.SemaphoreType.DMA((count,)),
            pltpu.SemaphoreType.DMA((count,)),
            pltpu.SemaphoreType.DMA((4,)),
        ],
        compiler_params=pltpu.CompilerParams(collective_id=0, has_side_effects=True),
    )(mixed, rows, down)


def gather_tokens(own):
    tokens, width = own.shape
    return pl.pallas_call(
        tokens_kernel,
        out_shape=jax.ShapeDtypeStruct((tokens, width * NY), own.dtype),
        in_specs=[spec(pltpu.VMEM)],
        out_specs=spec(pl.ANY),
        scratch_shapes=[
            pltpu.SemaphoreType.DMA((14,)),
            pltpu.SemaphoreType.DMA((14,)),
            pltpu.SemaphoreType.DMA((2,)),
        ],
        compiler_params=pltpu.CompilerParams(collective_id=1, has_side_effects=True),
        cost_estimate=pl.CostEstimate(flops=0, bytes_accessed=60_000_000, transcendentals=0),
    )(own)


def body(
    streams,
    doc_ids,
    doc_adapter,
    width_weights,
    stream_mixing,
    depth_static,
    depth_dir,
    qkv_weight,
    adapter_down,
    adapter_up,
    out_weight,
    page_slot,
):
    count_streams = streams.shape[0]
    tokens = streams.shape[1]
    mixed_local = width_weights[0] * streams[0].astype(jnp.float32)
    for stream in range(1, count_streams):
        mixed_local = mixed_local + width_weights[stream] * streams[stream].astype(jnp.float32)

    page_count = page_slot.shape[0]
    width_local = qkv_weight.shape[2]
    rows_local = qkv_weight.shape[0]
    groups = lax.axis_size("req")
    target_dev = page_slot // page_count
    local_slot = page_slot % page_count
    lane = jnp.arange(128)[None, :]
    labels = jnp.where(
        lane == 0, target_dev[:, None], jnp.where(lane == 1, local_slot[:, None], 0)
    ).astype(jnp.bfloat16)
    rows = jnp.concatenate([qkv_weight.reshape(rows_local, 3 * width_local), out_weight, labels], axis=1)
    gathered, rows_all, down_all = gather_all(
        mixed_local.astype(jnp.bfloat16), rows, adapter_down.transpose(0, 2, 1)
    )
    rows_all = rows_all.reshape(groups * rows_local, -1)
    qkv_all = rows_all[:, : 3 * width_local]
    out_all = rows_all[:, 3 * width_local : 4 * width_local]
    label_all = rows_all[:, 4 * width_local : 4 * width_local + 2].astype(jnp.int32)

    widened = gathered.astype(jnp.float32)
    normed = (
        widened * lax.rsqrt(jnp.mean(widened * widened, axis=-1, keepdims=True) + EPSILON)
    ).astype(jnp.bfloat16)
    segment = doc_ids[0]
    doc_table = doc_adapter[0, :, 0]
    token_adapter = jnp.sum(
        jnp.where(
            segment[:, None] == jnp.arange(doc_table.shape[0])[None, :], doc_table[None, :], 0
        ),
        axis=1,
    )
    adapters_total = adapter_up.shape[0]
    lanes = jnp.arange(adapters_total * R)[None, :]
    own_lane = token_adapter[:, None] == lanes // R
    every_rank = lax.dot_general(
        normed,
        down_all.reshape(adapters_total * R, -1),
        (((1,), (1,)), ((), ())),
        preferred_element_type=jnp.float32,
    )
    spread = jnp.where(own_lane, every_rank, 0.0).astype(jnp.bfloat16)
    lowrank = jnp.dot(
        spread, adapter_up.reshape(adapters_total * R, -1), preferred_element_type=jnp.float32
    )
    base = jnp.dot(normed, qkv_all, preferred_element_type=jnp.float32)
    heads_local = width_local // HD
    projected = (base + lowrank).astype(jnp.bfloat16)
    positions = jnp.arange(tokens)
    allowed = (segment[:, None] == segment[None, :]) & (positions[None, :] <= positions[:, None])
    parts = []
    for head in range(heads_local):
        query, key, value = (
            projected[:, part * width_local + head * HD : part * width_local + (head + 1) * HD]
            for part in range(3)
        )
        scores = lax.dot_general(
            query, key, (((1,), (1,)), ((), ())), preferred_element_type=jnp.float32
        ) / math.sqrt(HD)
        scores = jnp.where(allowed, scores, -1e30)
        highest = jnp.max(scores, axis=-1, keepdims=True)
        weights = jnp.exp(scores - highest)
        weights = (weights / jnp.sum(weights, axis=-1, keepdims=True)).astype(jnp.bfloat16)
        parts.append(jnp.dot(weights, value, preferred_element_type=jnp.float32).astype(jnp.bfloat16))
    attended = gather_tokens(jnp.concatenate(parts, axis=1))
    layer_out = jnp.dot(attended, out_all, preferred_element_type=jnp.float32)
    depth = depth_static[None, :] + jnp.tanh(
        jnp.dot(normed, depth_dir, preferred_element_type=jnp.float32)
    )
    outputs = []
    for stream in range(count_streams):
        carried = stream_mixing[stream, 0] * streams[0].astype(jnp.float32)
        for source in range(1, count_streams):
            carried = carried + stream_mixing[stream, source] * streams[source].astype(jnp.float32)
        outputs.append((carried + depth[:, stream][:, None] * layer_out).astype(jnp.bfloat16))
    new_streams = jnp.stack(outputs)

    cache = projected[:, width_local:].reshape(page_count, PAGE, 2, width_local)
    capacity = 2 * max(1, page_count // (2 * groups))
    ordinal = jnp.arange(page_count)
    earlier = (target_dev[None, :] == target_dev[:, None]) & (ordinal[None, :] < ordinal[:, None])
    placement = target_dev * capacity + jnp.sum(earlier.astype(jnp.int32), axis=1)
    outgoing = (
        jnp.zeros((groups * capacity, PAGE, 2, width_local), jnp.bfloat16).at[placement].set(cache)
    )
    incoming = lax.all_to_all(outgoing, "req", split_axis=0, concat_axis=0, tiled=True)
    came = (label_all[:, 0] == lax.axis_index("req")).reshape(groups, page_count)
    turn_in = jnp.cumsum(came.astype(jnp.int32), axis=1) - 1
    came_slot = label_all[:, 1].reshape(groups, page_count)
    slot_index = jnp.stack(
        [
            jnp.sum(jnp.where(came & (turn_in == number), came_slot + 1, 0), axis=1)
            for number in range(capacity)
        ],
        axis=1,
    ).reshape(-1)
    slot_index = jnp.where(slot_index == 0, page_count, slot_index - 1)
    kv_pool = (
        jnp.zeros((page_count + 1, PAGE, 2, width_local), jnp.bfloat16)
        .at[slot_index]
        .set(incoming)[:page_count]
    )
    return (new_streams, kv_pool)


def solution(mesh):
    in_specs = (
        P(None, "req", "wt"),
        P("req", None),
        P("req", None, None),
        P(),
        P(),
        P(),
        P(),
        P("req", None, "wt"),
        P("wt", None, None),
        P(None, None, None, "wt"),
        P("req", "wt"),
        P("req"),
    )
    out_specs = (P(None, "req", "wt"), P("req", None, None, "wt"))
    return jax.shard_map(body, mesh=mesh, in_specs=in_specs, out_specs=out_specs, check_vma=False)
```

time: 409 us -> 138 us (0.34)
  waiting for transfers between devices: 311 us -> 4.82 us
  Pallas kernels: 0 us -> 73.6 us
  starting transfers between devices: 21 us -> 4.44 us
  between operations: 14.1 us -> 0.97 us
  local copies, waits for them, and re-layouts: 23.4 us -> 17.3 us
    all_gather x4 -> x0, waiting for transfers between devices: 259 us -> none  [the longest x1 88.9 us: body(): portion = lax.all_gather(qkv_weight, 'req', axis=0, tiled=True)]
    pallas_call x0 -> x2, Pallas kernels: none -> 73.6 us  [the longest x1 49 us: gather_all(): pl.pallas_call(gather_kernel, out_shape=[jax.ShapeDtypeStruct((tokens, wi...]
    all_to_all x1, waiting for transfers between devices: 47.8 us -> 4.82 us  [body(): lax.all_to_all(outgoing, 'req', split_axis=0, concat_axis=0, tiled=True)]
    all_to_all x2 -> x0, starting transfers between devices: 12.8 us -> none  [the longest x1 6.46 us: body(): lax.all_to_all(every_row, 'wt', split_axis=0, concat_axis=1, tiled=True)]
    all_gather x1 -> x0, local copies, waits for them, and re-layouts: 4.73 us -> none  [body(): portion = lax.all_gather(qkv_weight, 'req', axis=0, tiled=True)]
    dot_general x3 -> x6, matrix products: 8.36 us -> 8.57 us  [the longest x1 5.07 us: body(): base = jnp.dot(normed, qkv_all, preferred_element_type=jnp.float32)]
  transfers between devices with their start and end apart: 8 -> 1, of which waited for: 6 -> 1; matrix products, arithmetic and copies ran while one was open for 8% -> 16% of each run, Pallas kernels for 0% -> 18%
where the time goes in v1:
time: 138 us
  Pallas kernels  73.6 us (53%)
  other arithmetic  22.5 us (16%)
  local copies, waits for them, and re-layouts  17.3 us (13%)
  matrix products  14 us (10%)
  waiting for transfers between devices  4.82 us (3%)
  starting transfers between devices  4.44 us (3%)
    pallas_call x1, Pallas kernels, gather_all(): pl.pallas_call(gather_kernel, out_shape=[jax.ShapeDtypeStruct((tokens, wi...  49 us
    pallas_call x1, Pallas kernels, gather_tokens(): pl.pallas_call(tokens_kernel, out_shape=jax.ShapeDtypeStruct((tokens, wid...  24.5 us
    another operation x3, other arithmetic, body(): new_streams = jnp.stack(outputs)  11.7 us
    dot_general x1, matrix products, body(): base = jnp.dot(normed, qkv_all, preferred_element_type=jnp.float32)  5.07 us
    all_to_all x1, waiting for transfers between devices, body(): lax.all_to_all(outgoing, 'req', split_axis=0, concat_axis=0, tiled=True)  4.82 us
    scatter x1, local copies, waits for them, and re-layouts, body(): kv_pool = jnp.zeros((page_count + 1, PAGE, 2, width_local), jnp.bfloat16)...  4.65 us
    convert_element_type x1, other arithmetic, body(): mixed_local.astype(jnp.bfloat16)  4.6 us
    all_to_all x1, starting transfers between devices, body(): lax.all_to_all(outgoing, 'req', split_axis=0, concat_axis=0, tiled=True)  4.44 us
  transfers between devices with their start and end apart: 1, of which 1 were waited for; matrix products, arithmetic and copies ran while one was open for 16% of the time, Pallas kernels for 18%

profile of v1, /device:TPU:1, one launch (start us, length us, event | category | flops | bytes accessed | tf_op | source)
XLA Modules:
  0.0 137.6 jit_solution(15734502700075556911)
XLA Ops:
  0.7 1.5 %fusion.66 = (f32[1]{0:T(128)}, f32[1]{0:T(128)}, f32[1]{0:T(128)}, f32[1]{0:T(128)}) fusion(f32[4]{0:T(128)} %param.15), kind=kLoop, calls=%fused_computation.126 | loop fusion | bytes 32 | tf_op jit(solution)/shard_map/slice | solution.py:276
  2.1 0.7 and_select_fusion.2
  2.8 0.8 copy.35
  3.9 1.4 pad_maximum_fusion.2.rows
  5.2 4.6 %fusion.42.mixed = bf16[512,256]{1,0:T(8,128)(2,1)} fusion(f32[]{:T(128)} %bitcast.8, f32[]{:T(128)} %bitcast.7, f32[]{:T(128)} %bitcast.6, f32[]{:T(128)} %bitcast.5, bf16[4,512,256]{2,1,0:T(8,128)(2,1)} %param.12), kind=kLoop, calls=%fused_computation.79 | loop fusion | flops 1572864 | bytes 1310736 | tf_op jit(solution)/shard_map/convert_element_type | solution.py:292
  9.8 49.0 %shard_map.131 = (bf16[512,2048]{1,0:T(8,128)(2,1)}, bf16[4,8,2,32,1152]{4,3,2,1,0:T(8,128)(2,1)}, bf16[8,2,16,2048]{3,2,1,0:T(8,128)(2,1)}) custom-call(bf16[512,256]{1,0:T(8,128)(2,1)} %fusion.42.mixed, bf16[32,1152]{1,0:T(8,128)(2,1)} %pad_maximum_fusion.2.rows, bf16[2,16,2048]{2,1,0:T(8,128)(2,1)} %bitcast.87), custom_call_target="tpu_custom_call" | custom-call | tf_op jit(solution)/shard_map/pallas_call | solution.py:225
  58.9 2.2 %fusion = f32[512]{0:T(512)S(1)} fusion(bf16[512,2048]{1,0:T(8,128)(2,1)} %get-tuple-element.5), kind=kLoop, calls=%fused_computation.4 | loop fusion | flops 3145216 | bytes 2099200 | tf_op jit(solution)/shard_map/reduce_sum | solution.py:301
  61.1 0.3 copy.25
  61.5 5.1 %fusion.2 = f32[512,768]{1,0:T(8,128)} fusion(bf16[2048,1152]{1,0:T(8,128)(2,1)} %bitcast.88, bf16[512,2048]{1,0:T(8,128)(2,1)S(1)} %copy-done.2, f32[512]{0:T(512)S(1)} %add_rsqrt_fusion), kind=kOutput, calls=%fused_computation.6 | convolution fusion | flops 1613758464 | bytes 6817792 | tf_op jit(solution)/shard_map/dot_general | solution.py:324
  66.7 3.1 %add_convert_fusion = bf16[512,768]{1,0:T(8,128)(2,1)S(1)} fusion(f32[512,768]{1,0:T(8,128)} %fusion.2, bf16[256,768]{1,0:T(8,128)(2,1)S(1)} %bitcast.85, bf16[256,2048]{1,0:T(8,128)(2,1)} %bitcast.102, s32[256]{0:T(256)S(1)} %and_select_fusion, s32[512]{0:T(512)S(1)} %select_reduce_fusion.2, bf16[512,2048]{1,0:T(8,128)(2,1)S(1)} %copy-done.3, ...), kind=kOutput, calls=%fused_computation.8 | convolution fusion | flops 742522880 | bytes 5903360 | tf_op jit(solution)/shard_map/dot_general | solution.py:321
  70.1 1.6 %broadcast_in_dim.106 = bf16[128,16,2,256]{3,1,2,0:T(8,128)(2,1)} broadcast(bf16[]{:T(256)} %constant.80.clone.1), dimensions={} | broadcast | bytes 2097154 | tf_op jit(solution)/shard_map/broadcast_in_dim | solution.py:362
  71.7 4.3 %scatter_fusion = bf16[128,16,2,256]{3,1,2,0:T(8,128)(2,1)} fusion(bf16[128,16,2,256]{3,1,2,0:T(8,128)(2,1)} %broadcast_in_dim.106, s32[32]{0:T(128)S(1)} %compare_select_fusion, bf16[32,16,2,256]{3,1,2,0:T(8,128)(2,1)S(1)} %copy.30), kind=kCustom, calls=%fused_computation | custom fusion | bytes 1572992 | tf_op jit(solution)/shard_map/scatter | solution.py:362
  76.0 4.4 %all-to-all-start = ((bf16[128,16,2,256]{3,1,2,0:T(8,128)(2,1)}), bf16[128,16,2,256]{3,1,2,0:T(8,128)(2,1)S(1)}, u32[]{:S(2)}, u32[]{:S(2)}) async-start(bf16[128,16,2,256]{3,1,2,0:T(8,128)(2,1)} %scatter_fusion), calls=%async_computation | async-start | bytes 4194304 | tf_op jit(solution)/shard_map/all_to_all | solution.py:364
  80.5 1.1 slice.192
  81.6 0.4 fusion.67
  81.9 0.2 fusion.12
  82.1 0.4 fusion.68
  82.5 0.2 fusion.11
  82.7 0.4 convolution_convert_fusion
  83.1 0.4 convolution_convert_fusion.1
  83.5 0.7 pad_maximum_fusion.1.own
  84.2 24.5 %shard_map.132 = bf16[512,2048]{1,0:T(8,128)(2,1)} custom-call(bf16[512,256]{1,0:T(8,128)(2,1)} %pad_maximum_fusion.1.own), custom_call_target="tpu_custom_call" | custom-call | bytes 60000000 | tf_op jit(solution)/shard_map/pallas_call | solution.py:245
  108.8 0.2 copy.34
  109.8 0.7 fusion.65
  110.6 2.3 %fusion.7 = f32[512,4]{0,1:T(4,128)S(1)} fusion(bf16[2048,4]{0,1:T(4,128)(2,1)S(1)} %copy-done, f32[4]{0:T(128)S(1)} %copy-done.9, bf16[512,2048]{1,0:T(8,128)(2,1)} %get-tuple-element.5, f32[512]{0:T(512)S(1)} %add_rsqrt_fusion), kind=kOutput, calls=%fused_computation.18 | convolution fusion | flops 11536384 | bytes 2123792 | tf_op jit(solution)/shard_map/dot_general | solution.py:346
  112.9 2.0 %fusion.8 = f32[512,256]{1,0:T(8,128)S(1)} fusion(bf16[512,2048]{1,0:T(8,128)(2,1)S(1)} %copy-done.4, bf16[2048,1152]{1,0:T(8,128)(2,1)} %bitcast.90), kind=kOutput, calls=%fused_computation.19 | convolution fusion | flops 536870912 | bytes 3670016 | tf_op jit(solution)/shard_map/dot_general | solution.py:344
  115.0 5.3 %fusion.49 = (bf16[1,512,256]{2,1,0:T(8,128)(2,1)S(1)}, bf16[1,512,256]{2,1,0:T(8,128)(2,1)S(1)}) fusion(f32[512,256]{1,0:T(8,128)S(1)} %fusion.8, f32[512]{0:T(512)S(1)} %bitcast.94, f32[]{:T(128)} %bitcast.3, f32[]{:T(128)} %bitcast.2, f32[]{:T(128)} %bitcast.1, f32[]{:T(128)} %bitcast, bf16[4,512,256]{2,1,0:T(8,128)(2,1)S(1)} %copy-done.1, ...), kind=kLoop, calls=%fused_computation.87 | loop fusion | flops 3145728 | bytes 2101280 | tf_op jit(solution)/shard_map/stack | solution.py:354
  120.3 5.3 %fusion.48 = (bf16[1,512,256]{2,1,0:T(8,128)(2,1)S(1)}, bf16[1,512,256]{2,1,0:T(8,128)(2,1)S(1)}) fusion(f32[512,256]{1,0:T(8,128)S(1)} %fusion.8, f32[512]{0:T(512)S(1)} %bitcast.93, f32[]{:T(128)} %bitcast.20, f32[]{:T(128)} %bitcast.19, f32[]{:T(128)} %bitcast.18, f32[]{:T(128)} %bitcast.17, bf16[4,512,256]{2,1,0:T(8,128)(2,1)S(1)} %copy-done.1, ...), kind=kLoop, calls=%fused_computation.86 | loop fusion | flops 3145728 | bytes 2101280 | tf_op jit(solution)/shard_map/stack | solution.py:354
  125.6 1.1 pad_maximum_fusion
  126.7 4.8 %all-to-all-done = bf16[128,16,2,256]{3,1,2,0:T(8,128)(2,1)S(1)} async-done(((bf16[128,16,2,256]{3,1,2,0:T(8,128)(2,1)}), bf16[128,16,2,256]{3,1,2,0:T(8,128)(2,1)S(1)}, u32[]{:S(2)}, u32[]{:S(2)}) %all-to-all-start) | async-done | bytes 2097184 | tf_op jit(solution)/shard_map/all_to_all | solution.py:364
  131.6 4.6 %scatter_fusion.1 = bf16[33,16,2,256]{3,1,2,0:T(8,128)(2,1)S(1)} fusion(bf16[33,16,2,256]{3,1,2,0:T(8,128)(2,1)S(1)} %broadcast_in_dim.104, s32[128]{0:T(128)S(1)} %fusion.58, bf16[128,16,2,256]{3,1,2,0:T(8,128)(2,1)S(1)} %all-to-all-done), kind=kCustom, calls=%fused_computation.1 | custom fusion | bytes 6291968 | tf_op jit(solution)/shard_map/scatter | solution.py:379
  136.3 1.3 copy.31
  (46 shorter events, 1.7 us)
Async XLA Ops:
  0.6 109.9 %copy-start = (bf16[2048,4]{0,1:T(4,128)(2,1)S(1)}, bf16[2048,4]{0,1:T(4,128)(2,1)}, u32[]{:S(2)}) copy-start(bf16[2048,4]{0,1:T(4,128)(2,1)} %param.18) | copy-start | bytes 49156
  0.6 60.5 %copy-start.5 = (bf16[16,16,3,256]{3,1,2,0:T(8,128)(2,1)S(1)}, bf16[16,16,3,256]{3,1,2,0:T(8,128)(2,1)}, u32[]{:S(2)}) copy-start(bf16[16,16,3,256]{3,1,2,0:T(8,128)(2,1)} %param.21) | copy-start | bytes 1179652
  58.9 2.6 %copy-start.2 = (bf16[512,2048]{1,0:T(8,128)(2,1)S(1)}, bf16[512,2048]{1,0:T(8,128)(2,1)}, u32[]{:S(2)}) copy-start(bf16[512,2048]{1,0:T(8,128)(2,1)} %get-tuple-element.5) | copy-start | bytes 6291460
  61.5 5.1 %copy-start.7 = (s32[1,512]{1,0:T(1,128)S(1)}, s32[1,512]{1,0:T(1,128)}, u32[]{:S(2)}) copy-start(s32[1,512]{1,0:T(1,128)} %param.13) | copy-start | bytes 6148
  61.5 5.1 %copy-start.8 = (s32[1,4,1]{1,2,0:T(1,128)S(1)}, s32[1,4,1]{1,2,0:T(1,128)}, u32[]{:S(2)}) copy-start(s32[1,4,1]{1,2,0:T(1,128)} %param.14) | copy-start | bytes 52
  61.5 5.2 %copy-start.3 = (bf16[512,2048]{1,0:T(8,128)(2,1)S(1)}, bf16[512,2048]{1,0:T(8,128)(2,1)}, u32[]{:S(2)}) copy-start(bf16[512,2048]{1,0:T(8,128)(2,1)} %get-tuple-element.5) | copy-start | bytes 6291460
  76.0 55.5 %all-to-all-start = ((bf16[128,16,2,256]{3,1,2,0:T(8,128)(2,1)}), bf16[128,16,2,256]{3,1,2,0:T(8,128)(2,1)S(1)}, u32[]{:S(2)}, u32[]{:S(2)}) async-start(bf16[128,16,2,256]{3,1,2,0:T(8,128)(2,1)} %scatter_fusion), calls=%async_computation | async-start | bytes 4194304 | tf_op jit(solution)/shard_map/all_to_all | solution.py:364
  83.5 26.3 %copy-start.6 = (f32[4,4]{1,0:T(4,128)S(1)}, f32[4,4]{1,0:T(4,128)}, u32[]{:S(2)}) copy-start(f32[4,4]{1,0:T(4,128)} %param.16) | copy-start | bytes 196
  83.5 27.1 %copy-start.9 = (f32[4]{0:T(128)S(1)}, f32[4]{0:T(128)}, u32[]{:S(2)}) copy-start(f32[4]{0:T(128)} %param.17) | copy-start | bytes 52
  109.8 3.1 %copy-start.4 = (bf16[512,2048]{1,0:T(8,128)(2,1)S(1)}, bf16[512,2048]{1,0:T(8,128)(2,1)}, u32[]{:S(2)}) copy-start(bf16[512,2048]{1,0:T(8,128)(2,1)} %shard_map.132) | copy-start | bytes 6291460
  112.9 2.0 %copy-start.1 = (bf16[4,512,256]{2,1,0:T(8,128)(2,1)S(1)}, bf16[4,512,256]{2,1,0:T(8,128)(2,1)}, u32[]{:S(2)}) copy-start(bf16[4,512,256]{2,1,0:T(8,128)(2,1)} %param.12) | copy-start | bytes 3145732

commit v2 on v1

--- a/solution.py
+++ b/solution.py
@@ -81,7 +81,9 @@
     held[key] = copies.start(src, columns(out, half, origin), req, turn(wt, direction, NY))
 
 
-def gather_kernel(mixed, rows, down, mixed_all, rows_all, down_all, send_sem, recv_sem, local_sem):
+def gather_kernel(
+    mixed, rows, out_rows, down, mixed_all, rows_all, out_all, down_all, send_sem, recv_sem, local_sem
+):
     req, wt, x, z, core = position()
     partner = req + 1 - 2 * core
 
@@ -99,7 +101,11 @@
         + [(near_x(1), wt), (near_x(-1), wt), (near_z(1), wt), (near_z(-1), wt)]
     )
     copies = Copies(send_sem, recv_sem)
-    held_tokens, held_down, held_rows = {}, {}, {}
+    held_tokens, held_down, held_rows, held_out = {}, {}, {}, {}
+    slice_width = down.shape[2] // NX
+
+    def down_lanes(x_at):
+        return pl.ds(pl.multiple_of(x_at * slice_width, slice_width), slice_width)
 
     def rows_hop(unit, direction, step):
         if step == 3 and unit % 2 != (0 if direction == 1 else 1):
@@ -111,14 +117,27 @@
         src = rows if (step == 0 and unit == 0) else block
         held_rows[key] = copies.start(src, block, near_z(direction), wt)
 
-    def down_hop(direction, step):
-        if step == 3 and direction == -1:
-            return
-        if step > 0:
-            held_down[direction].wait_recv()
-        block = down_all.at[turn(wt, -direction * step, NY), core]
-        src = down.at[core] if step == 0 else block
-        held_down[direction] = copies.start(src, block, req, turn(wt, direction, NY))
+    def token_step(half, step):
+        for direction in (1, -1):
+            token_hop(copies, held_tokens, mixed, mixed_all, req, wt, half, direction, step)
+
+    def small_hop(step):
+        for direction in (1, -1):
+            if step == 3 and direction == -1:
+                continue
+            if step > 0:
+                held_down[direction].wait_recv()
+                held_out[direction].wait_recv()
+            block = down_all.at[turn(wt, -direction * step, NY), core, :, down_lanes(x)]
+            src = down.at[core, :, down_lanes(x)] if step == 0 else block
+            held_down[direction] = copies.start(src, block, req, turn(wt, direction, NY))
+            block = out_all.at[x, turn(z, -direction * step, NZ), core]
+            src = out_rows if step == 0 else block
+            held_out[direction] = copies.start(src, block, near_z(direction), wt)
+
+    def small_blocks(shift):
+        x_at = turn(x, shift, NX)
+        return down_all.at[:, core, :, down_lanes(x_at)], out_all.at[x_at, :, core]
 
     def share(z_shift):
         block = rows_all.at[:, turn(z, z_shift, NZ), core]
@@ -127,19 +146,20 @@
     own_rows = rows_all.at[x, z, core]
     from_left = copies.start(rows, own_rows, near_x(1), wt)
     from_right = copies.start(rows, own_rows, near_x(-1), wt)
+    small_hop(0)
+    token_step(0, 0)
     for direction in (1, -1):
-        token_hop(copies, held_tokens, mixed, mixed_all, req, wt, 0, direction, 0)
         rows_hop(0, direction, 0)
-    for direction in (1, -1):
-        token_hop(copies, held_tokens, mixed, mixed_all, req, wt, 1, direction, 0)
-        down_hop(direction, 0)
+    token_step(1, 0)
+    half = mixed.shape[0] // 2
     locals_ = [
         pltpu.make_async_copy(rows, own_rows, local_sem.at[0]),
-        pltpu.make_async_copy(mixed.at[pl.ds(0, mixed.shape[0] // 2)], columns(mixed_all, 0, wt), local_sem.at[1]),
+        pltpu.make_async_copy(mixed.at[pl.ds(0, half)], columns(mixed_all, 0, wt), local_sem.at[1]),
+        pltpu.make_async_copy(mixed.at[pl.ds(half, half)], columns(mixed_all, 1, wt), local_sem.at[2]),
         pltpu.make_async_copy(
-            mixed.at[pl.ds(mixed.shape[0] // 2, mixed.shape[0] // 2)], columns(mixed_all, 1, wt), local_sem.at[2]
+            down.at[core, :, down_lanes(x)], down_all.at[wt, core, :, down_lanes(x)], local_sem.at[3]
         ),
-        pltpu.make_async_copy(down.at[core], down_all.at[wt, core], local_sem.at[3]),
+        pltpu.make_async_copy(out_rows, out_all.at[x, z, core], local_sem.at[4]),
     ]
     for copy in locals_:
         copy.start()
@@ -157,27 +177,42 @@
     for copy in locals_:
         copy.wait()
     shared = [share(0)]
+    small_left, small_right, small_far = [], [], []
     for step in range(1, 4):
         for unit in (0, 1, 3, 2):
             for direction in (1, -1):
                 rows_hop(unit, direction, step)
-            if unit == 1 or unit == 2:
+            if unit == 1:
+                token_step(0, step)
+            if unit == 2:
+                token_step(1, step)
+            if (step, unit) == (1, 0):
+                small_hop(1)
+            if (step, unit) == (1, 3):
+                small_hop(2)
+            if (step, unit) == (2, 0):
+                small_hop(3)
+            if (step, unit) == (2, 3):
                 for direction in (1, -1):
-                    token_hop(
-                        copies, held_tokens, mixed, mixed_all, req, wt, 0 if unit == 1 else 1, direction, step
-                    )
+                    held_down[direction].wait_recv()
+                    held_out[direction].wait_recv()
+                for block in small_blocks(0):
+                    small_left.append(copies.start(block, block, near_x(1), wt))
+                    small_right.append(copies.start(block, block, near_x(-1), wt))
+            if (step, unit) == (3, 0):
+                for copy, block in zip(small_left, small_blocks(-1)):
+                    copy.wait_recv()
+                    small_far.append(copies.start(block, block, near_x(1), wt))
         if step == 3:
             for unit in (1, 3):
                 held_rows[(unit, 1)].wait_recv()
             for unit in (0, 2):
                 held_rows[(unit, -1)].wait_recv()
-        for direction in (1, -1):
-            down_hop(direction, step)
         shared += [share(-step), share(step)]
-    held_down[-1].wait_recv()
-    held_down[1].wait_recv()
-    every_down = down_all.at[:, core]
-    shared.append(copies.start(every_down, every_down, partner, wt))
+    for copy in small_right + small_far:
+        copy.wait_recv()
+    for block in (down_all.at[:, core], out_all.at[:, :, core]):
+        shared.append(copies.start(block, block, partner, wt))
     for unit in (0, 2):
         held_rows[(unit, 1)].wait_recv()
     for unit in (1, 3):
@@ -219,25 +254,114 @@
     return pl.BlockSpec(memory_space=space)
 
 
-def gather_all(mixed, rows, down):
+def gather_all(mixed, rows, out_rows, down):
     tokens, width = mixed.shape
-    count = 3 + 28 + 8 + 14 + 7 + 1
+    count = 3 + 28 + 8 + 14 + 2 * (7 + 3 + 1)
     return pl.pallas_call(
         gather_kernel,
         out_shape=[
             jax.ShapeDtypeStruct((tokens, width * NY), mixed.dtype),
             jax.ShapeDtypeStruct((NX, NZ, NC) + rows.shape, rows.dtype),
+            jax.ShapeDtypeStruct((NX, NZ, NC) + out_rows.shape, out_rows.dtype),
             jax.ShapeDtypeStruct((NY,) + down.shape, down.dtype),
         ],
-        in_specs=[spec(pltpu.VMEM)] * 3,
-        out_specs=[spec(pl.ANY)] * 3,
+        in_specs=[spec(pltpu.VMEM)] * 4,
+        out_specs=[spec(pl.ANY)] * 4,
         scratch_shapes=[
             pltpu.SemaphoreType.DMA((count,)),
             pltpu.SemaphoreType.DMA((count,)),
-            pltpu.SemaphoreType.DMA((4,)),
+            pltpu.SemaphoreType.DMA((5,)),
         ],
         compiler_params=pltpu.CompilerParams(collective_id=0, has_side_effects=True),
-    )(mixed, rows, down)
+    )(mixed, rows, out_rows, down)
+
+
+def mixed_kernel(weights, streams, out):
+    total = weights[0] * streams[0].astype(jnp.float32)
+    for stream in range(1, streams.shape[0]):
+        total = total + weights[stream] * streams[stream].astype(jnp.float32)
+    out[...] = total.astype(out.dtype)
+
+
+def mix_in(width_weights, streams):
+    count, tokens, width = streams.shape
+    block = tokens // 2
+    return pl.pallas_call(
+        mixed_kernel,
+        grid=(tokens // block,),
+        out_shape=jax.ShapeDtypeStruct((tokens, width), streams.dtype),
+        in_specs=[spec(pltpu.SMEM), pl.BlockSpec((count, block, width), lambda i: (0, i, 0))],
+        out_specs=pl.BlockSpec((block, width), lambda i: (i, 0)),
+    )(width_weights, streams)
+
+
+def pack_kernel(placement, cache, out, sem):
+    started = []
+    for page in range(cache.shape[0]):
+        started.append(pltpu.make_async_copy(cache.at[page], out.at[placement[page]], sem.at[page]))
+        started[-1].start()
+    for copy in started:
+        copy.wait()
+
+
+def pack(placement, cache, slots):
+    return pl.pallas_call(
+        pack_kernel,
+        out_shape=jax.ShapeDtypeStruct((slots,) + cache.shape[1:], cache.dtype),
+        in_specs=[spec(pltpu.SMEM), spec(pltpu.VMEM)],
+        out_specs=spec(pl.ANY),
+        scratch_shapes=[pltpu.SemaphoreType.DMA((cache.shape[0],))],
+    )(placement, cache)
+
+
+def unpack_kernel(chosen, incoming, out, sem):
+    started = []
+    for page in range(out.shape[0]):
+        started.append(pltpu.make_async_copy(incoming.at[chosen[page]], out.at[page], sem.at[page]))
+        started[-1].start()
+    for copy in started:
+        copy.wait()
+
+
+def unpack(chosen, incoming):
+    pages = chosen.shape[0]
+    return pl.pallas_call(
+        unpack_kernel,
+        out_shape=jax.ShapeDtypeStruct((pages,) + incoming.shape[1:], incoming.dtype),
+        in_specs=[spec(pltpu.SMEM), spec(pl.ANY)],
+        out_specs=spec(pltpu.VMEM),
+        scratch_shapes=[pltpu.SemaphoreType.DMA((pages,))],
+    )(chosen, incoming)
+
+
+def finish_kernel(mixing, attended, weight, depth, streams, out):
+    layer_out = jnp.dot(attended[...], weight[...], preferred_element_type=jnp.float32)
+    count = streams.shape[0]
+    wide = [streams[source].astype(jnp.float32) for source in range(count)]
+    for stream in range(count):
+        carried = mixing[stream, 0] * wide[0]
+        for source in range(1, count):
+            carried = carried + mixing[stream, source] * wide[source]
+        out[stream] = (carried + depth[:, stream : stream + 1] * layer_out).astype(out.dtype)
+
+
+def finish(stream_mixing, attended, weight, depth, streams):
+    count, tokens, width = streams.shape
+    block = tokens // 4
+    return pl.pallas_call(
+        finish_kernel,
+        grid=(tokens // block,),
+        out_shape=jax.ShapeDtypeStruct(streams.shape, streams.dtype),
+        in_specs=[
+            spec(pltpu.SMEM),
+            pl.BlockSpec((block, attended.shape[1]), lambda i: (i, 0)),
+            pl.BlockSpec(weight.shape, lambda i: (0, 0)),
+            pl.BlockSpec((block, count), lambda i: (i, 0)),
+            pl.BlockSpec((count, block, width), lambda i: (0, i, 0)),
+        ],
+        out_specs=pl.BlockSpec((count, block, width), lambda i: (0, i, 0)),
+        cost_estimate=pl.CostEstimate(flops=600_000_000, bytes_accessed=6_000_000, transcendentals=0),
+    )(stream_mixing, attended, weight, depth, streams)
 
 
 def gather_tokens(own):
@@ -273,28 +397,36 @@
 ):
     count_streams = streams.shape[0]
     tokens = streams.shape[1]
-    mixed_local = width_weights[0] * streams[0].astype(jnp.float32)
-    for stream in range(1, count_streams):
-        mixed_local = mixed_local + width_weights[stream] * streams[stream].astype(jnp.float32)
-
     page_count = page_slot.shape[0]
     width_local = qkv_weight.shape[2]
     rows_local = qkv_weight.shape[0]
     groups = lax.axis_size("req")
     target_dev = page_slot // page_count
     local_slot = page_slot % page_count
+    capacity = 2 * max(1, page_count // (2 * groups))
+    ordinal = jnp.arange(page_count)
+    earlier = (target_dev[None, :] == target_dev[:, None]) & (ordinal[None, :] < ordinal[:, None])
+    place = jnp.sum(earlier.astype(jnp.int32), axis=1)
+    placement = target_dev * capacity + place
     lane = jnp.arange(128)[None, :]
     labels = jnp.where(
-        lane == 0, target_dev[:, None], jnp.where(lane == 1, local_slot[:, None], 0)
+        lane == 0,
+        target_dev[:, None],
+        jnp.where(lane == 1, local_slot[:, None], jnp.where(lane == 2, place[:, None], 0)),
     ).astype(jnp.bfloat16)
-    rows = jnp.concatenate([qkv_weight.reshape(rows_local, 3 * width_local), out_weight, labels], axis=1)
-    gathered, rows_all, down_all = gather_all(
-        mixed_local.astype(jnp.bfloat16), rows, adapter_down.transpose(0, 2, 1)
+    rows = jnp.concatenate([qkv_weight.reshape(rows_local, 3 * width_local), labels], axis=1)
+    gathered, rows_all, out_all, down_all = gather_all(
+        mix_in(width_weights, streams), rows, out_weight, adapter_down.transpose(0, 2, 1)
     )
     rows_all = rows_all.reshape(groups * rows_local, -1)
+    out_all = out_all.reshape(groups * rows_local, width_local)
     qkv_all = rows_all[:, : 3 * width_local]
-    out_all = rows_all[:, 3 * width_local : 4 * width_local]
-    label_all = rows_all[:, 4 * width_local : 4 * width_local + 2].astype(jnp.int32)
+    label_all = rows_all[:, 3 * width_local : 3 * width_local + 3].astype(jnp.int32)
+    came = label_all[:, 0] == lax.axis_index("req")
+    came_row = (jnp.arange(groups * page_count) // page_count) * capacity + label_all[:, 2]
+    chosen = jnp.sum(
+        jnp.where(came[None, :] & (label_all[:, 1][None, :] == ordinal[:, None]), came_row[None, :], 0), axis=1
+    )
 
     widened = gathered.astype(jnp.float32)
     normed = (
@@ -341,43 +473,15 @@
         weights = (weights / jnp.sum(weights, axis=-1, keepdims=True)).astype(jnp.bfloat16)
         parts.append(jnp.dot(weights, value, preferred_element_type=jnp.float32).astype(jnp.bfloat16))
     attended = gather_tokens(jnp.concatenate(parts, axis=1))
-    layer_out = jnp.dot(attended, out_all, preferred_element_type=jnp.float32)
     depth = depth_static[None, :] + jnp.tanh(
         jnp.dot(normed, depth_dir, preferred_element_type=jnp.float32)
     )
-    outputs = []
-    for stream in range(count_streams):
-        carried = stream_mixing[stream, 0] * streams[0].astype(jnp.float32)
-        for source in range(1, count_streams):
-            carried = carried + stream_mixing[stream, source] * streams[source].astype(jnp.float32)
-        outputs.append((carried + depth[:, stream][:, None] * layer_out).astype(jnp.bfloat16))
-    new_streams = jnp.stack(outputs)
-
-    cache = projected[:, width_local:].reshape(page_count, PAGE, 2, width_local)
-    capacity = 2 * max(1, page_count // (2 * groups))
-    ordinal = jnp.arange(page_count)
-    earlier = (target_dev[None, :] == target_dev[:, None]) & (ordinal[None, :] < ordinal[:, None])
-    placement = target_dev * capacity + jnp.sum(earlier.astype(jnp.int32), axis=1)
-    outgoing = (
-        jnp.zeros((groups * capacity, PAGE, 2, width_local), jnp.bfloat16).at[placement].set(cache)
-    )
+    new_streams = finish(stream_mixing, attended, out_all, depth, streams)
+
+    cache = projected[:, width_local:].reshape(page_count, PAGE, 2 * width_local)
+    outgoing = pack(placement, cache, groups * capacity)
     incoming = lax.all_to_all(outgoing, "req", split_axis=0, concat_axis=0, tiled=True)
-    came = (label_all[:, 0] == lax.axis_index("req")).reshape(groups, page_count)
-    turn_in = jnp.cumsum(came.astype(jnp.int32), axis=1) - 1
-    came_slot = label_all[:, 1].reshape(groups, page_count)
-    slot_index = jnp.stack(
-        [
-            jnp.sum(jnp.where(came & (turn_in == number), came_slot + 1, 0), axis=1)
-            for number in range(capacity)
-        ],
-        axis=1,
-    ).reshape(-1)
-    slot_index = jnp.where(slot_index == 0, page_count, slot_index - 1)
-    kv_pool = (
-        jnp.zeros((page_count + 1, PAGE, 2, width_local), jnp.bfloat16)
-        .at[slot_index]
-        .set(incoming)[:page_count]
-    )
+    kv_pool = unpack(chosen, incoming).reshape(page_count, PAGE, 2, width_local)
     return (new_streams, kv_pool)
 
 

time: 138 us -> 134 us (0.971)
  other arithmetic: 22.5 us -> 6.25 us
  Pallas kernels: 73.6 us -> 88.3 us
  local copies, waits for them, and re-layouts: 17.3 us -> 7.62 us
  waiting for transfers between devices: 4.82 us -> 13.4 us
  matrix products: 14 us -> 12.6 us
    another operation x4 -> x0, other arithmetic: 11.9 us -> none  [the longest x3 11.7 us: body(): new_streams = jnp.stack(outputs)]
    pallas_call x0 -> x4, Pallas kernels: none -> 11.8 us  [the longest x1 4.89 us: finish(): pl.pallas_call(finish_kernel, grid=(tokens // block,), out_shape=jax.Shap...]
    scatter x2 -> x0, local copies, waits for them, and re-layouts: 8.98 us -> none  [the longest x1 4.65 us: body(): kv_pool = jnp.zeros((page_count + 1, PAGE, 2, width_local), jnp.bfloat16)...]
    all_to_all x1, waiting for transfers between devices: 4.82 us -> 13.4 us  [body(): lax.all_to_all(outgoing, 'req', split_axis=0, concat_axis=0, tiled=True)]
    convert_element_type x3 -> x1, other arithmetic: 4.62 us -> 0.02 us  [body(): rows_all[:, 3 * width_local:3 * width_local + 3].astype(jnp.int32)]
    pallas_call x1, Pallas kernels: 49 us -> 51.5 us  [gather_all(): pl.pallas_call(gather_kernel, out_shape=[jax.ShapeDtypeStruct((tokens, wi...]
    dot_general x1 -> x0, matrix products: 2.02 us -> none  [body(): layer_out = jnp.dot(attended, out_all, preferred_element_type=jnp.float32)]
    reshape x2 -> x1, local copies, waits for them, and re-layouts: 0.21 us -> 1.96 us  [body(): kv_pool = unpack(chosen, incoming).reshape(page_count, PAGE, 2, width_local)]
  transfers between devices with their start and end apart: 1 -> 1, of which waited for: 1 -> 1; matrix products, arithmetic and copies ran while one was open for 16% -> 6% of each run, Pallas kernels for 18% -> 22%
where the time goes in v2:
time: 134 us; the launch traced here: 133 us
  Pallas kernels  88.3 us (66%)
  waiting for transfers between devices  13.4 us (10%)
  matrix products  12.6 us (9%)
  local copies, waits for them, and re-layouts  7.62 us (6%)
  other arithmetic  6.25 us (5%)
  starting transfers between devices  4.35 us (3%)
    pallas_call x1, Pallas kernels, gather_all(): pl.pallas_call(gather_kernel, out_shape=[jax.ShapeDtypeStruct((tokens, wi...  51.5 us
    pallas_call x1, Pallas kernels, gather_tokens(): pl.pallas_call(tokens_kernel, out_shape=jax.ShapeDtypeStruct((tokens, wid...  25.1 us
    all_to_all x1, waiting for transfers between devices, body(): lax.all_to_all(outgoing, 'req', split_axis=0, concat_axis=0, tiled=True)  13.4 us
    dot_general x1, matrix products, body(): base = jnp.dot(normed, qkv_all, preferred_element_type=jnp.float32)  4.96 us
    pallas_call x1, Pallas kernels, finish(): pl.pallas_call(finish_kernel, grid=(tokens // block,), out_shape=jax.Shap...  4.89 us
    all_to_all x1, starting transfers between devices, body(): lax.all_to_all(outgoing, 'req', split_axis=0, concat_axis=0, tiled=True)  4.35 us
    dot_general x1, matrix products, body(): jnp.dot(spread, adapter_up.reshape(adapters_total * R, -1), preferred_ele...  3.09 us
    dot_general x1, matrix products, body(): jnp.dot(normed, depth_dir, preferred_element_type=jnp.float32)  3.06 us
  transfers between devices with their start and end apart: 1, of which 1 were waited for; matrix products, arithmetic and copies ran while one was open for 6% of the time, Pallas kernels for 22%

profile of v2, /device:TPU:1, one launch (start us, length us, event | category | flops | bytes accessed | tf_op | source)
XLA Modules:
  0.0 133.4 jit_solution(16587627117953058333)
XLA Ops:
  0.7 0.7 and_select_fusion.1
  1.3 0.2 convert_reduce_fusion
  1.5 0.5 multiply_add_fusion.placement
  2.0 0.8 copy.41
  2.8 1.3 copy.31
  4.3 0.6 pad_maximum_fusion.1.rows
  4.9 2.0 %shard_map.131.mixed = bf16[512,256]{1,0:T(8,128)(2,1)} custom-call(f32[4]{0:T(128)} %weights.1, bf16[4,512,256]{2,1,0:T(8,128)(2,1)} %streams.3), custom_call_target="tpu_custom_call" | custom-call | tf_op jit(solution)/shard_map/pallas_call | solution.py:289
  6.9 51.5 %shard_map.132 = (bf16[512,2048]{1,0:T(8,128)(2,1)}, bf16[4,8,2,32,896]{4,3,2,1,0:T(8,128)(2,1)}, bf16[4,8,2,32,256]{4,3,2,1,0:T(8,128)(2,1)}, bf16[8,2,16,2048]{3,2,1,0:T(8,128)(2,1)}) custom-call(bf16[512,256]{1,0:T(8,128)(2,1)} %shard_map.131.mixed, bf16[32,896]{1,0:T(8,128)(2,1)} %pad_maximum_fusion.1.rows, bf16[32,256]{1,0:T(8,128)(2,1)} %out_rows.1, ...), custom_call_target="tpu_custom_call" | custom-call | tf_op jit(solution)/shard_map/pallas_call | solution.py:260
  58.4 2.2 %fusion = f32[512]{0:T(512)S(1)} fusion(bf16[512,2048]{1,0:T(8,128)(2,1)} %get-tuple-element.6), kind=kLoop, calls=%fused_computation.2 | loop fusion | flops 3145216 | bytes 2099200 | tf_op jit(solution)/shard_map/reduce_sum | solution.py:433
  60.6 0.1 select_reduce_fusion.1
  60.7 5.0 %fusion.2 = f32[512,768]{1,0:T(8,128)} fusion(bf16[2048,896]{1,0:T(8,128)(2,1)} %bitcast.23, bf16[512,2048]{1,0:T(8,128)(2,1)S(1)} %copy-done.2, f32[512]{0:T(512)S(1)} %add_rsqrt_fusion), kind=kOutput, calls=%fused_computation.4 | convolution fusion | flops 1613758464 | bytes 6817792 | tf_op jit(solution)/shard_map/dot_general | solution.py:456
  65.7 3.1 %add_convert_fusion = bf16[512,768]{1,0:T(8,128)(2,1)S(1)} fusion(f32[512,768]{1,0:T(8,128)} %fusion.2, bf16[256,768]{1,0:T(8,128)(2,1)S(1)} %bitcast.20, bf16[256,2048]{1,0:T(8,128)(2,1)} %bitcast.32, s32[256]{0:T(256)S(1)} %and_select_fusion, s32[512]{0:T(512)S(1)} %select_reduce_fusion.1, bf16[512,2048]{1,0:T(8,128)(2,1)S(1)} %copy-done.2, ...), kind=kOutput, calls=%fused_computation.6 | convolution fusion | flops 742522880 | bytes 5903360 | tf_op jit(solution)/shard_map/dot_general | solution.py:453
  68.7 0.8 slice.59
  69.6 2.2 %shard_map.135 = bf16[128,16,512]{2,1,0:T(8,128)(2,1)} custom-call(s32[32]{0:T(128)} %multiply_add_fusion.placement, bf16[32,16,512]{2,1,0:T(8,128)(2,1)} %bitcast.18), custom_call_target="tpu_custom_call" | custom-call | tf_op jit(solution)/shard_map/pallas_call | solution.py:308
  71.7 4.3 %all-to-all-start = ((bf16[128,16,512]{2,1,0:T(8,128)(2,1)}), bf16[128,16,512]{2,1,0:T(8,128)(2,1)S(1)}, u32[]{:S(2)}, u32[]{:S(2)}) async-start(bf16[128,16,512]{2,1,0:T(8,128)(2,1)} %shard_map.135), calls=%async_computation | async-start | bytes 4194304 | tf_op jit(solution)/shard_map/all_to_all | solution.py:483
  76.1 1.1 slice.55
  77.2 0.2 copy.40
  77.4 0.4 fusion.34
  77.8 0.2 fusion.10
  78.0 0.4 fusion.35
  78.4 0.2 fusion.9
  78.6 0.4 convolution_convert_fusion
  78.9 0.4 convolution_convert_fusion.1
  79.3 0.7 pad_maximum_fusion.own
  80.1 25.1 %shard_map.133.attended = bf16[512,2048]{1,0:T(8,128)(2,1)} custom-call(bf16[512,256]{1,0:T(8,128)(2,1)} %pad_maximum_fusion.own), custom_call_target="tpu_custom_call" | custom-call | bytes 60000000 | tf_op jit(solution)/shard_map/pallas_call | solution.py:369
  105.2 3.1 %fusion.7.depth = f32[512,4]{1,0:T(8,128)} fusion(bf16[2048,4]{0,1:T(4,128)(2,1)S(1)} %copy-done, f32[4]{0:T(128)S(1)} %copy-done.5, bf16[512,2048]{1,0:T(8,128)(2,1)} %get-tuple-element.6, f32[512]{0:T(512)S(1)} %add_rsqrt_fusion), kind=kOutput, calls=%fused_computation.14 | convolution fusion | flops 11536384 | bytes 2123792 | tf_op jit(solution)/shard_map/dot_general | solution.py:477
  108.2 4.9 %shard_map.134 = bf16[4,512,256]{2,1,0:T(8,128)(2,1)} custom-call(f32[4,4]{1,0:T(4,128)} %mixing.1, bf16[512,2048]{1,0:T(8,128)(2,1)} %shard_map.133.attended, bf16[2048,256]{1,0:T(8,128)(2,1)} %bitcast.19, f32[512,4]{1,0:T(8,128)} %fusion.7.depth, bf16[4,512,256]{2,1,0:T(8,128)(2,1)} %streams.3), custom_call_target="tpu_custom_call" | custom-call | flops 600000000 | bytes 6000000 | tf_op jit(solution)/shard_map/pallas_call | solution.py:351
  113.2 0.7 select_reduce_fusion.chosen
  113.9 13.4 %all-to-all-done.incoming = bf16[128,16,512]{2,1,0:T(8,128)(2,1)S(1)} async-done(((bf16[128,16,512]{2,1,0:T(8,128)(2,1)}), bf16[128,16,512]{2,1,0:T(8,128)(2,1)S(1)}, u32[]{:S(2)}, u32[]{:S(2)}) %all-to-all-start) | async-done | bytes 2097184 | tf_op jit(solution)/shard_map/all_to_all | solution.py:483
  127.3 1.3 %copy-done.1 = bf16[128,16,512]{2,1,0:T(8,128)(2,1)} copy-done((bf16[128,16,512]{2,1,0:T(8,128)(2,1)}, bf16[128,16,512]{2,1,0:T(8,128)(2,1)S(1)}, u32[]{:S(2)}) %copy-start.1) | copy-done | bytes 2097176
  128.7 2.7 %shard_map.136 = bf16[32,16,512]{2,1,0:T(8,128)(2,1)} custom-call(s32[32]{0:T(128)} %select_reduce_fusion.chosen, bf16[128,16,512]{2,1,0:T(8,128)(2,1)} %copy-done.1), custom_call_target="tpu_custom_call" | custom-call | tf_op jit(solution)/shard_map/pallas_call | solution.py:328
  131.4 2.0 %reshape.130 = bf16[32,16,2,256]{3,2,1,0:T(2,128)(2,1)} reshape(bf16[32,16,512]{2,1,0:T(8,128)(2,1)} %shard_map.136) | data formatting | bytes 1048576 | tf_op jit(solution)/shard_map/reshape | solution.py:484
  (21 shorter events, 0.3 us)
Async XLA Ops:
  0.6 104.5 %copy-start = (bf16[2048,4]{0,1:T(4,128)(2,1)S(1)}, bf16[2048,4]{0,1:T(4,128)(2,1)}, u32[]{:S(2)}) copy-start(bf16[2048,4]{0,1:T(4,128)(2,1)} %param.18) | copy-start | bytes 49156
  4.2 56.4 %copy-start.3 = (s32[1,512]{1,0:T(1,128)S(1)}, s32[1,512]{1,0:T(1,128)}, u32[]{:S(2)}) copy-start(s32[1,512]{1,0:T(1,128)} %param.13) | copy-start | bytes 6148
  4.2 56.4 %copy-start.4 = (s32[1,4,1]{1,2,0:T(1,128)S(1)}, s32[1,4,1]{1,2,0:T(1,128)}, u32[]{:S(2)}) copy-start(s32[1,4,1]{1,2,0:T(1,128)} %param.14) | copy-start | bytes 52
  58.3 2.4 %copy-start.2 = (bf16[512,2048]{1,0:T(8,128)(2,1)S(1)}, bf16[512,2048]{1,0:T(8,128)(2,1)}, u32[]{:S(2)}) copy-start(bf16[512,2048]{1,0:T(8,128)(2,1)} %get-tuple-element.6) | copy-start | bytes 6291460
  71.7 55.6 %all-to-all-start = ((bf16[128,16,512]{2,1,0:T(8,128)(2,1)}), bf16[128,16,512]{2,1,0:T(8,128)(2,1)S(1)}, u32[]{:S(2)}, u32[]{:S(2)}) async-start(bf16[128,16,512]{2,1,0:T(8,128)(2,1)} %shard_map.135), calls=%async_computation | async-start | bytes 4194304 | tf_op jit(solution)/shard_map/all_to_all | solution.py:483
  79.3 25.8 %copy-start.5 = (f32[4]{0:T(128)S(1)}, f32[4]{0:T(128)}, u32[]{:S(2)}) copy-start(f32[4]{0:T(128)} %param.17) | copy-start | bytes 52
  127.3 1.4 %copy-start.1 = (bf16[128,16,512]{2,1,0:T(8,128)(2,1)}, bf16[128,16,512]{2,1,0:T(8,128)(2,1)S(1)}, u32[]{:S(2)}) copy-start(bf16[128,16,512]{2,1,0:T(8,128)(2,1)S(1)} %all-to-all-done.incoming) | copy-start | bytes 6291460

commit v3 on v2

--- a/solution.py
+++ b/solution.py
@@ -97,129 +97,103 @@
         return at(x, turn(z, shift, NZ))
 
     meet(
-        [(req, turn(wt, 1, NY)), (req, turn(wt, -1, NY)), (partner, wt)]
-        + [(near_x(1), wt), (near_x(-1), wt), (near_z(1), wt), (near_z(-1), wt)]
+        [(partner, wt)]
+        + [(req, turn(wt, shift, NY)) for shift in range(1, NY)]
+        + [(near_z(shift), wt) for shift in range(1, NZ)]
+        + [(near_x(shift), wt) for shift in range(1, NX)]
     )
     copies = Copies(send_sem, recv_sem)
-    held_tokens, held_down, held_rows, held_out = {}, {}, {}, {}
+    held_tokens, held_rows = {}, {}
     slice_width = down.shape[2] // NX
+    both = (1, -1)
 
     def down_lanes(x_at):
         return pl.ds(pl.multiple_of(x_at * slice_width, slice_width), slice_width)
 
-    def rows_hop(unit, direction, step):
-        if step == 3 and unit % 2 != (0 if direction == 1 else 1):
-            return
-        key = (unit, direction)
-        if step > 0:
-            held_rows[key].wait_recv()
-        block = rows_all.at[turn(x, -unit, NX), turn(z, -direction * step, NZ), core]
-        src = rows if (step == 0 and unit == 0) else block
-        held_rows[key] = copies.start(src, block, near_z(direction), wt)
+    def rows_hop(unit, step):
+        for direction in both:
+            if step == 3 and unit % 2 != (0 if direction == 1 else 1):
+                continue
+            key = (unit, direction)
+            if step > 0:
+                held_rows[key].wait_recv()
+            block = rows_all.at[turn(x, -unit, NX), turn(z, -direction * step, NZ), core]
+            src = rows if (step == 0 and unit == 0) else block
+            held_rows[key] = copies.start(src, block, near_z(direction), wt)
 
     def token_step(half, step):
-        for direction in (1, -1):
+        for direction in both:
             token_hop(copies, held_tokens, mixed, mixed_all, req, wt, half, direction, step)
-
-    def small_hop(step):
-        for direction in (1, -1):
-            if step == 3 and direction == -1:
-                continue
-            if step > 0:
-                held_down[direction].wait_recv()
-                held_out[direction].wait_recv()
-            block = down_all.at[turn(wt, -direction * step, NY), core, :, down_lanes(x)]
-            src = down.at[core, :, down_lanes(x)] if step == 0 else block
-            held_down[direction] = copies.start(src, block, req, turn(wt, direction, NY))
-            block = out_all.at[x, turn(z, -direction * step, NZ), core]
-            src = out_rows if step == 0 else block
-            held_out[direction] = copies.start(src, block, near_z(direction), wt)
-
-    def small_blocks(shift):
-        x_at = turn(x, shift, NX)
-        return down_all.at[:, core, :, down_lanes(x_at)], out_all.at[x_at, :, core]
 
     def share(z_shift):
         block = rows_all.at[:, turn(z, z_shift, NZ), core]
         return copies.start(block, block, partner, wt)
 
     own_rows = rows_all.at[x, z, core]
-    from_left = copies.start(rows, own_rows, near_x(1), wt)
-    from_right = copies.start(rows, own_rows, near_x(-1), wt)
-    small_hop(0)
+    own_out = out_all.at[x, z, core]
+    own_down = down_all.at[wt, core, :, down_lanes(x)]
+    small = []
+    for shift in (1, 7, 2, 6, 3, 5, 4):
+        small.append(copies.start(out_rows, own_out, near_z(shift), wt))
+        small.append(copies.start(down.at[core, :, down_lanes(x)], own_down, req, turn(wt, shift, NY)))
+    along_x = {shift: copies.start(rows, own_rows, near_x(shift), wt) for shift in (1, 3, 2)}
     token_step(0, 0)
-    for direction in (1, -1):
-        rows_hop(0, direction, 0)
+    rows_hop(0, 0)
     token_step(1, 0)
     half = mixed.shape[0] // 2
     locals_ = [
         pltpu.make_async_copy(rows, own_rows, local_sem.at[0]),
         pltpu.make_async_copy(mixed.at[pl.ds(0, half)], columns(mixed_all, 0, wt), local_sem.at[1]),
         pltpu.make_async_copy(mixed.at[pl.ds(half, half)], columns(mixed_all, 1, wt), local_sem.at[2]),
-        pltpu.make_async_copy(
-            down.at[core, :, down_lanes(x)], down_all.at[wt, core, :, down_lanes(x)], local_sem.at[3]
-        ),
-        pltpu.make_async_copy(out_rows, out_all.at[x, z, core], local_sem.at[4]),
+        pltpu.make_async_copy(down.at[core, :, down_lanes(x)], own_down, local_sem.at[3]),
+        pltpu.make_async_copy(out_rows, own_out, local_sem.at[4]),
     ]
     for copy in locals_:
         copy.start()
-    from_left.wait_recv()
-    left_block = rows_all.at[turn(x, -1, NX), z, core]
-    far = copies.start(left_block, left_block, near_x(1), wt)
-    for direction in (1, -1):
-        rows_hop(1, direction, 0)
-    from_right.wait_recv()
-    for direction in (1, -1):
-        rows_hop(3, direction, 0)
-    far.wait_recv()
-    for direction in (1, -1):
-        rows_hop(2, direction, 0)
+    for shift in (1, 3, 2):
+        along_x[shift].wait_recv()
+        rows_hop(shift, 0)
     for copy in locals_:
         copy.wait()
     shared = [share(0)]
-    small_left, small_right, small_far = [], [], []
-    for step in range(1, 4):
-        for unit in (0, 1, 3, 2):
-            for direction in (1, -1):
-                rows_hop(unit, direction, step)
-            if unit == 1:
-                token_step(0, step)
-            if unit == 2:
-                token_step(1, step)
-            if (step, unit) == (1, 0):
-                small_hop(1)
-            if (step, unit) == (1, 3):
-                small_hop(2)
-            if (step, unit) == (2, 0):
-                small_hop(3)
-            if (step, unit) == (2, 3):
-                for direction in (1, -1):
-                    held_down[direction].wait_recv()
-                    held_out[direction].wait_recv()
-                for block in small_blocks(0):
-                    small_left.append(copies.start(block, block, near_x(1), wt))
-                    small_right.append(copies.start(block, block, near_x(-1), wt))
-            if (step, unit) == (3, 0):
-                for copy, block in zip(small_left, small_blocks(-1)):
-                    copy.wait_recv()
-                    small_far.append(copies.start(block, block, near_x(1), wt))
-        if step == 3:
-            for unit in (1, 3):
-                held_rows[(unit, 1)].wait_recv()
-            for unit in (0, 2):
-                held_rows[(unit, -1)].wait_recv()
-        shared += [share(-step), share(step)]
-    for copy in small_right + small_far:
+    rows_hop(0, 1)
+    for copy in small:
+        copy.wait_recv()
+    down_block, out_block = down_all.at[:, core, :, down_lanes(x)], out_all.at[x, :, core]
+    small = []
+    for shift in (1, 3, 2):
+        for block in (down_block, out_block):
+            small.append(copies.start(block, block, near_x(shift), wt))
+    for unit in (1, 3, 2):
+        rows_hop(unit, 1)
+    shared += [share(-1), share(1)]
+    token_step(0, 1)
+    rows_hop(0, 2)
+    rows_hop(1, 2)
+    token_step(1, 1)
+    rows_hop(3, 2)
+    rows_hop(2, 2)
+    shared += [share(-2), share(2)]
+    rows_hop(0, 3)
+    token_step(0, 2)
+    rows_hop(1, 3)
+    rows_hop(3, 3)
+    token_step(1, 2)
+    rows_hop(2, 3)
+    for copy in small:
         copy.wait_recv()
     for block in (down_all.at[:, core], out_all.at[:, :, core]):
         shared.append(copies.start(block, block, partner, wt))
-    for unit in (0, 2):
-        held_rows[(unit, 1)].wait_recv()
-    for unit in (1, 3):
-        held_rows[(unit, -1)].wait_recv()
+    token_step(0, 3)
+    for key in ((1, 1), (3, 1), (0, -1), (2, -1)):
+        held_rows[key].wait_recv()
+    shared += [share(-3), share(3)]
+    for key in ((0, 1), (2, 1), (1, -1), (3, -1)):
+        held_rows[key].wait_recv()
     shared.append(share(4))
+    token_step(1, 3)
     for half in (0, 1):
-        for direction in (1, -1):
+        for direction in both:
             held_tokens[(half, direction)].wait_recv()
     for copy in shared:
         copy.wait_recv()
@@ -314,13 +288,9 @@
     )(placement, cache)
 
 
-def unpack_kernel(chosen, incoming, out, sem):
-    started = []
+def unpack_kernel(chosen, incoming, out):
     for page in range(out.shape[0]):
-        started.append(pltpu.make_async_copy(incoming.at[chosen[page]], out.at[page], sem.at[page]))
-        started[-1].start()
-    for copy in started:
-        copy.wait()
+        out[page] = incoming[chosen[page]]
 
 
 def unpack(chosen, incoming):
@@ -328,9 +298,8 @@
     return pl.pallas_call(
         unpack_kernel,
         out_shape=jax.ShapeDtypeStruct((pages,) + incoming.shape[1:], incoming.dtype),
-        in_specs=[spec(pltpu.SMEM), spec(pl.ANY)],
+        in_specs=[spec(pltpu.SMEM), spec(pltpu.VMEM)],
         out_specs=spec(pltpu.VMEM),
-        scratch_shapes=[pltpu.SemaphoreType.DMA((pages,))],
     )(chosen, incoming)
 
 
@@ -450,20 +419,24 @@
         preferred_element_type=jnp.float32,
     )
     spread = jnp.where(own_lane, every_rank, 0.0).astype(jnp.bfloat16)
-    lowrank = jnp.dot(
-        spread, adapter_up.reshape(adapters_total * R, -1), preferred_element_type=jnp.float32
-    )
-    base = jnp.dot(normed, qkv_all, preferred_element_type=jnp.float32)
+    up = adapter_up.reshape(adapters_total * R, -1)
+
+    def project(start, stop):
+        base = jnp.dot(normed, qkv_all[:, start:stop], preferred_element_type=jnp.float32)
+        lowrank = jnp.dot(spread, up[:, start:stop], preferred_element_type=jnp.float32)
+        return (base + lowrank).astype(jnp.bfloat16)
+
     heads_local = width_local // HD
-    projected = (base + lowrank).astype(jnp.bfloat16)
+    cache = project(width_local, 3 * width_local)
+    queries = project(0, width_local)
     positions = jnp.arange(tokens)
     allowed = (segment[:, None] == segment[None, :]) & (positions[None, :] <= positions[:, None])
     parts = []
     for head in range(heads_local):
-        query, key, value = (
-            projected[:, part * width_local + head * HD : part * width_local + (head + 1) * HD]
-            for part in range(3)
-        )
+        at = head * HD
+        query = queries[:, at : at + HD]
+        key = cache[:, at : at + HD]
+        value = cache[:, width_local + at : width_local + at + HD]
         scores = lax.dot_general(
             query, key, (((1,), (1,)), ((), ())), preferred_element_type=jnp.float32
         ) / math.sqrt(HD)
@@ -478,8 +451,7 @@
     )
     new_streams = finish(stream_mixing, attended, out_all, depth, streams)
 
-    cache = projected[:, width_local:].reshape(page_count, PAGE, 2 * width_local)
-    outgoing = pack(placement, cache, groups * capacity)
+    outgoing = pack(placement, cache.reshape(page_count, PAGE, 2 * width_local), groups * capacity)
     incoming = lax.all_to_all(outgoing, "req", split_axis=0, concat_axis=0, tiled=True)
     kv_pool = unpack(chosen, incoming).reshape(page_count, PAGE, 2, width_local)
     return (new_streams, kv_pool)

time: 134 us -> 126 us (0.940)
  Pallas kernels: 88.3 us -> 80.7 us
  starting transfers between devices: 4.35 us -> 8.47 us
  waiting for transfers between devices: 13.4 us -> 10.3 us
    pallas_call x1, Pallas kernels: 51.5 us -> 43.8 us  [gather_all(): pl.pallas_call(gather_kernel, out_shape=[jax.ShapeDtypeStruct((tokens, wi...]
    all_to_all x1, starting transfers between devices: 4.35 us -> 8.47 us  [body(): lax.all_to_all(outgoing, 'req', split_axis=0, concat_axis=0, tiled=True)]
    all_to_all x1, waiting for transfers between devices: 13.4 us -> 10.3 us  [body(): lax.all_to_all(outgoing, 'req', split_axis=0, concat_axis=0, tiled=True)]
    dot_general x2 -> x5, matrix products: 8.04 us -> 7.7 us  [the longest x2 5.63 us: project(): jnp.dot(normed, qkv_all[:, start:stop], preferred_element_type=jnp.float32)]
    unnamed x15 -> x19, local copies, waits for them, and re-layouts: 2.94 us -> 2.95 us
  transfers between devices with their start and end apart: 1 -> 1, of which waited for: 1 -> 1; matrix products, arithmetic and copies ran while one was open for 6% -> 8% of each run, Pallas kernels for 22% -> 24%
where the time goes in v3:
time: 126 us
  Pallas kernels  80.7 us (64%)
  matrix products  12.3 us (10%)
  waiting for transfers between devices  10.3 us (8%)
  starting transfers between devices  8.47 us (7%)
  local copies, waits for them, and re-layouts  6.8 us (5%)
  other arithmetic  6.31 us (5%)
    pallas_call x1, Pallas kernels, gather_all(): pl.pallas_call(gather_kernel, out_shape=[jax.ShapeDtypeStruct((tokens, wi...  43.8 us
    pallas_call x1, Pallas kernels, gather_tokens(): pl.pallas_call(tokens_kernel, out_shape=jax.ShapeDtypeStruct((tokens, wid...  25.4 us
    all_to_all x1, waiting for transfers between devices, body(): lax.all_to_all(outgoing, 'req', split_axis=0, concat_axis=0, tiled=True)  10.3 us
    all_to_all x1, starting transfers between devices, body(): lax.all_to_all(outgoing, 'req', split_axis=0, concat_axis=0, tiled=True)  8.47 us
    dot_general x2, matrix products, project(): jnp.dot(normed, qkv_all[:, start:stop], preferred_element_type=jnp.float32)  5.63 us
    pallas_call x1, Pallas kernels, finish(): pl.pallas_call(finish_kernel, grid=(tokens // block,), out_shape=jax.Shap...  4.89 us
    dot_general x1, matrix products, body(): jnp.dot(normed, depth_dir, preferred_element_type=jnp.float32)  3.05 us
    unnamed x19, local copies, waits for them, and re-layouts  2.95 us
  transfers between devices with their start and end apart: 1, of which 1 were waited for; matrix products, arithmetic and copies ran while one was open for 8% of the time, Pallas kernels for 24%

profile of v3, /device:TPU:1, one launch (start us, length us, event | category | flops | bytes accessed | tf_op | source)
XLA Modules:
  0.0 125.7 jit_solution(17265383251449299365)
XLA Ops:
  0.7 0.7 and_select_fusion.1
  1.5 0.5 multiply_add_fusion.placement
  2.1 0.8 copy.41
  2.9 1.3 %copy.31 = bf16[16,16,3,256]{3,2,1,0:T(4,128)(2,1)S(1)} copy(bf16[16,16,3,256]{3,1,2,0:T(8,128)(2,1)} %param.21) | data formatting | bytes 786432 | tf_op args[9]
  4.3 0.6 pad_maximum_fusion.1.rows
  5.0 2.0 %shard_map.131.mixed = bf16[512,256]{1,0:T(8,128)(2,1)} custom-call(f32[4]{0:T(128)} %weights.1, bf16[4,512,256]{2,1,0:T(8,128)(2,1)} %streams.3), custom_call_target="tpu_custom_call" | custom-call | tf_op jit(solution)/shard_map/pallas_call | solution.py:263
  6.9 43.8 %shard_map.132 = (bf16[512,2048]{1,0:T(8,128)(2,1)}, bf16[4,8,2,32,896]{4,3,2,1,0:T(8,128)(2,1)}, bf16[4,8,2,32,256]{4,3,2,1,0:T(8,128)(2,1)}, bf16[8,2,16,2048]{3,2,1,0:T(8,128)(2,1)}) custom-call(bf16[512,256]{1,0:T(8,128)(2,1)} %shard_map.131.mixed, bf16[32,896]{1,0:T(8,128)(2,1)} %pad_maximum_fusion.1.rows, bf16[32,256]{1,0:T(8,128)(2,1)} %out_rows.1, ...), custom_call_target="tpu_custom_call" | custom-call | tf_op jit(solution)/shard_map/pallas_call | solution.py:234
  50.8 2.2 %fusion = f32[512]{0:T(512)S(1)} fusion(bf16[512,2048]{1,0:T(8,128)(2,1)} %get-tuple-element.6), kind=kLoop, calls=%fused_computation.2 | loop fusion | flops 3145216 | bytes 2099200 | tf_op jit(solution)/shard_map/reduce_sum | solution.py:402
  53.1 3.0 %fusion.2 = f32[512,512]{1,0:T(8,128)S(1)} fusion(bf16[2048,896]{1,0:T(8,128)(2,1)} %bitcast.25, bf16[512,2048]{1,0:T(8,128)(2,1)S(1)} %copy-done.2, f32[512]{0:T(512)S(1)} %add_rsqrt_fusion), kind=kOutput, calls=%fused_computation.4 | convolution fusion | flops 1076887552 | bytes 5244928 | tf_op jit(solution)/shard_map/dot_general | solution.py:425
  56.1 0.8 fusion.8
  56.9 1.1 fusion.6
  58.0 2.2 %shard_map.135 = bf16[128,16,512]{2,1,0:T(8,128)(2,1)} custom-call(s32[32]{0:T(128)} %multiply_add_fusion.placement, bf16[32,16,512]{2,1,0:T(8,128)(2,1)} %bitcast.19), custom_call_target="tpu_custom_call" | custom-call | tf_op jit(solution)/shard_map/pallas_call | solution.py:282
  60.1 8.5 %all-to-all-start = ((bf16[128,16,512]{2,1,0:T(8,128)(2,1)}), bf16[128,16,512]{2,1,0:T(8,128)(2,1)S(1)}, u32[]{:S(2)}, u32[]{:S(2)}) async-start(bf16[128,16,512]{2,1,0:T(8,128)(2,1)} %shard_map.135), calls=%async_computation | async-start | bytes 4194304 | tf_op jit(solution)/shard_map/all_to_all | solution.py:455
  68.6 1.1 slice.69
  69.7 0.2 copy.40
  70.0 0.2 fusion.22
  70.2 2.7 %fusion.7 = bf16[512,256]{1,0:T(8,128)(2,1)S(1)} fusion(f32[512,256]{1,0:T(8,128)S(1)} %fusion.22, bf16[2048,896]{1,0:T(8,128)(2,1)} %bitcast.27, bf16[512,2048]{1,0:T(8,128)(2,1)} %get-tuple-element.6, f32[512]{0:T(512)S(1)} %add_rsqrt_fusion), kind=kOutput, calls=%fused_computation.14 | convolution fusion | flops 540278784 | bytes 3934208 | tf_op jit(solution)/shard_map/dot_general | solution.py:425
  72.9 0.4 fusion.35
  73.2 0.2 fusion.13
  73.4 0.4 fusion.36
  73.8 0.2 fusion.12
  74.0 0.4 convolution_convert_fusion
  74.4 0.4 convolution_convert_fusion.1
  74.8 0.7 pad_maximum_fusion.own
  75.5 25.4 %shard_map.133.attended = bf16[512,2048]{1,0:T(8,128)(2,1)} custom-call(bf16[512,256]{1,0:T(8,128)(2,1)} %pad_maximum_fusion.own), custom_call_target="tpu_custom_call" | custom-call | bytes 60000000 | tf_op jit(solution)/shard_map/pallas_call | solution.py:338
  100.9 3.1 %fusion.9.depth = f32[512,4]{1,0:T(8,128)} fusion(bf16[2048,4]{0,1:T(4,128)(2,1)S(1)} %copy-done, f32[4]{0:T(128)S(1)} %copy-done.7, bf16[512,2048]{1,0:T(8,128)(2,1)} %get-tuple-element.6, f32[512]{0:T(512)S(1)} %add_rsqrt_fusion), kind=kOutput, calls=%fused_computation.17 | convolution fusion | flops 11536384 | bytes 2123792 | tf_op jit(solution)/shard_map/dot_general | solution.py:450
  104.0 4.9 %shard_map.134 = bf16[4,512,256]{2,1,0:T(8,128)(2,1)} custom-call(f32[4,4]{1,0:T(4,128)} %mixing.1, bf16[512,2048]{1,0:T(8,128)(2,1)} %shard_map.133.attended, bf16[2048,256]{1,0:T(8,128)(2,1)} %bitcast.22, f32[512,4]{1,0:T(8,128)} %fusion.9.depth, bf16[4,512,256]{2,1,0:T(8,128)(2,1)} %streams.3), custom_call_target="tpu_custom_call" | custom-call | flops 600000000 | bytes 6000000 | tf_op jit(solution)/shard_map/pallas_call | solution.py:320
  108.9 0.7 select_reduce_fusion.chosen
  109.6 10.3 %all-to-all-done.incoming = bf16[128,16,512]{2,1,0:T(8,128)(2,1)S(1)} async-done(((bf16[128,16,512]{2,1,0:T(8,128)(2,1)}), bf16[128,16,512]{2,1,0:T(8,128)(2,1)S(1)}, u32[]{:S(2)}, u32[]{:S(2)}) %all-to-all-start) | async-done | bytes 2097184 | tf_op jit(solution)/shard_map/all_to_all | solution.py:455
  119.9 1.3 %copy-done.1 = bf16[128,16,512]{2,1,0:T(8,128)(2,1)} copy-done((bf16[128,16,512]{2,1,0:T(8,128)(2,1)}, bf16[128,16,512]{2,1,0:T(8,128)(2,1)S(1)}, u32[]{:S(2)}) %copy-start.1) | copy-done | bytes 2097176
  121.3 2.4 %shard_map.136 = bf16[32,16,512]{2,1,0:T(8,128)(2,1)} custom-call(s32[32]{0:T(128)} %select_reduce_fusion.chosen, bf16[128,16,512]{2,1,0:T(8,128)(2,1)} %copy-done.1), custom_call_target="tpu_custom_call" | custom-call | tf_op jit(solution)/shard_map/pallas_call | solution.py:298
  123.7 2.0 %reshape.130 = bf16[32,16,2,256]{3,2,1,0:T(2,128)(2,1)} reshape(bf16[32,16,512]{2,1,0:T(8,128)(2,1)} %shard_map.136) | data formatting | bytes 1048576 | tf_op jit(solution)/shard_map/reshape | solution.py:456
  (27 shorter events, 0.6 us)
Async XLA Ops:
  0.6 100.3 %copy-start = (bf16[2048,4]{0,1:T(4,128)(2,1)S(1)}, bf16[2048,4]{0,1:T(4,128)(2,1)}, u32[]{:S(2)}) copy-start(bf16[2048,4]{0,1:T(4,128)(2,1)} %param.18) | copy-start | bytes 49156
  4.2 48.8 %copy-start.4 = (s32[1,512]{1,0:T(1,128)S(1)}, s32[1,512]{1,0:T(1,128)}, u32[]{:S(2)}) copy-start(s32[1,512]{1,0:T(1,128)} %param.13) | copy-start | bytes 6148
  4.2 48.8 %copy-start.5 = (s32[1,4,1]{1,2,0:T(1,128)S(1)}, s32[1,4,1]{1,2,0:T(1,128)}, u32[]{:S(2)}) copy-start(s32[1,4,1]{1,2,0:T(1,128)} %param.14) | copy-start | bytes 52
  50.8 2.4 %copy-start.2 = (bf16[512,2048]{1,0:T(8,128)(2,1)S(1)}, bf16[512,2048]{1,0:T(8,128)(2,1)}, u32[]{:S(2)}) copy-start(bf16[512,2048]{1,0:T(8,128)(2,1)} %get-tuple-element.6) | copy-start | bytes 6291460
  53.1 3.0 %copy-start.6 = (bf16[8,2,16,2048]{3,2,1,0:T(8,128)(2,1)S(1)}, bf16[8,2,16,2048]{3,2,1,0:T(8,128)(2,1)}, u32[]{:S(2)}) copy-start(bf16[8,2,16,2048]{3,2,1,0:T(8,128)(2,1)} %get-tuple-element.8) | copy-start | bytes 3145732
  60.1 59.8 %all-to-all-start = ((bf16[128,16,512]{2,1,0:T(8,128)(2,1)}), bf16[128,16,512]{2,1,0:T(8,128)(2,1)S(1)}, u32[]{:S(2)}, u32[]{:S(2)}) async-start(bf16[128,16,512]{2,1,0:T(8,128)(2,1)} %shard_map.135), calls=%async_computation | async-start | bytes 4194304 | tf_op jit(solution)/shard_map/all_to_all | solution.py:455
  70.2 2.7 %copy-start.3 = (bf16[512,512]{1,0:T(8,128)(2,1)S(1)}, bf16[512,512]{1,0:T(8,128)(2,1)}, u32[]{:S(2)}) copy-start(bf16[512,512]{1,0:T(8,128)(2,1)} %fusion.6) | copy-start | bytes 1572868
  74.8 26.1 %copy-start.7 = (f32[4]{0:T(128)S(1)}, f32[4]{0:T(128)}, u32[]{:S(2)}) copy-start(f32[4]{0:T(128)} %param.17) | copy-start | bytes 52
  119.9 1.4 %copy-start.1 = (bf16[128,16,512]{2,1,0:T(8,128)(2,1)}, bf16[128,16,512]{2,1,0:T(8,128)(2,1)S(1)}, u32[]{:S(2)}) copy-start(bf16[128,16,512]{2,1,0:T(8,128)(2,1)S(1)} %all-to-all-done.incoming) | copy-start | bytes 6291460

commit v4 on v3

--- a/solution.py
+++ b/solution.py
@@ -250,23 +250,43 @@
     )(mixed, rows, out_rows, down)
 
 
-def mixed_kernel(weights, streams, out):
+def mixed_kernel(weights, streams, qkv, labels, out, rows):
     total = weights[0] * streams[0].astype(jnp.float32)
     for stream in range(1, streams.shape[0]):
         total = total + weights[stream] * streams[stream].astype(jnp.float32)
     out[...] = total.astype(out.dtype)
 
-
-def mix_in(width_weights, streams):
+    @pl.when(pl.program_id(0) == 0)
+    def _():
+        width = qkv.shape[2]
+        block = qkv[...]
+        for part in range(3):
+            rows[:, part * width : (part + 1) * width] = block[:, part, :]
+        rows[:, 3 * width :] = labels[...]
+
+
+def mix_in(width_weights, streams, qkv, labels):
     count, tokens, width = streams.shape
     block = tokens // 2
+    row_shape = (qkv.shape[0], 3 * qkv.shape[2] + labels.shape[1])
     return pl.pallas_call(
         mixed_kernel,
         grid=(tokens // block,),
-        out_shape=jax.ShapeDtypeStruct((tokens, width), streams.dtype),
-        in_specs=[spec(pltpu.SMEM), pl.BlockSpec((count, block, width), lambda i: (0, i, 0))],
-        out_specs=pl.BlockSpec((block, width), lambda i: (i, 0)),
-    )(width_weights, streams)
+        out_shape=[
+            jax.ShapeDtypeStruct((tokens, width), streams.dtype),
+            jax.ShapeDtypeStruct(row_shape, qkv.dtype),
+        ],
+        in_specs=[
+            spec(pltpu.SMEM),
+            pl.BlockSpec((count, block, width), lambda i: (0, i, 0)),
+            pl.BlockSpec(qkv.shape, lambda i: (0, 0, 0)),
+            pl.BlockSpec(labels.shape, lambda i: (0, 0)),
+        ],
+        out_specs=[
+            pl.BlockSpec((block, width), lambda i: (i, 0)),
+            pl.BlockSpec(row_shape, lambda i: (0, 0)),
+        ],
+    )(width_weights, streams, qkv, labels)
 
 
 def pack_kernel(placement, cache, out, sem):
@@ -345,7 +365,9 @@
             pltpu.SemaphoreType.DMA((14,)),
             pltpu.SemaphoreType.DMA((2,)),
         ],
-        compiler_params=pltpu.CompilerParams(collective_id=1, has_side_effects=True),
+        compiler_params=pltpu.CompilerParams(
+            collective_id=1, has_side_effects=True, vmem_limit_bytes=66_000_000
+        ),
         cost_estimate=pl.CostEstimate(flops=0, bytes_accessed=60_000_000, transcendentals=0),
     )(own)
 
@@ -383,9 +405,9 @@
         target_dev[:, None],
         jnp.where(lane == 1, local_slot[:, None], jnp.where(lane == 2, place[:, None], 0)),
     ).astype(jnp.bfloat16)
-    rows = jnp.concatenate([qkv_weight.reshape(rows_local, 3 * width_local), labels], axis=1)
+    mixed_local, rows = mix_in(width_weights, streams, qkv_weight, labels)
     gathered, rows_all, out_all, down_all = gather_all(
-        mix_in(width_weights, streams), rows, out_weight, adapter_down.transpose(0, 2, 1)
+        mixed_local, rows, out_weight, adapter_down.transpose(0, 2, 1)
     )
     rows_all = rows_all.reshape(groups * rows_local, -1)
     out_all = out_all.reshape(groups * rows_local, width_local)

time: 126 us -> 126 us (level)
    unnamed x19 -> x18, local copies, waits for them, and re-layouts: 2.95 us -> 3.08 us
where the time goes in v4:
time: 126 us
  Pallas kernels  80 us (63%)
  matrix products  11.6 us (9%)
  waiting for transfers between devices  11.5 us (9%)
  starting transfers between devices  9.27 us (7%)
  other arithmetic  6.24 us (5%)
  local copies, waits for them, and re-layouts  6.13 us (5%)
    pallas_call x1, Pallas kernels, gather_all(): pl.pallas_call(gather_kernel, out_shape=[jax.ShapeDtypeStruct((tokens, wi...  43.8 us
    pallas_call x1, Pallas kernels, gather_tokens(): pl.pallas_call(tokens_kernel, out_shape=jax.ShapeDtypeStruct((tokens, wid...  24.7 us
    all_to_all x1, waiting for transfers between devices, body(): lax.all_to_all(outgoing, 'req', split_axis=0, concat_axis=0, tiled=True)  11.5 us
    all_to_all x1, starting transfers between devices, body(): lax.all_to_all(outgoing, 'req', split_axis=0, concat_axis=0, tiled=True)  9.27 us
    dot_general x2, matrix products, project(): jnp.dot(normed, qkv_all[:, start:stop], preferred_element_type=jnp.float32)  5 us
    pallas_call x1, Pallas kernels, finish(): pl.pallas_call(finish_kernel, grid=(tokens // block,), out_shape=jax.Shap...  4.89 us
    unnamed x18, local copies, waits for them, and re-layouts  3.08 us
    dot_general x1, matrix products, body(): jnp.dot(normed, depth_dir, preferred_element_type=jnp.float32)  3.06 us
  transfers between devices with their start and end apart: 1, of which 1 were waited for; matrix products, arithmetic and copies ran while one was open for 8% of the time, Pallas kernels for 24%

profile of v4, /device:TPU:1, one launch (start us, length us, event | category | flops | bytes accessed | tf_op | source)
XLA Modules:
  0.0 125.7 jit_solution(18128755668998696870)
XLA Ops:
  0.7 0.7 and_select_fusion.1
  1.3 0.2 convert_reduce_fusion
  1.5 0.5 multiply_add_fusion.placement
  2.0 1.5 %copy.30.qkv = bf16[32,3,256]{2,1,0:T(4,128)(2,1)} copy(bf16[32,3,256]{2,0,1:T(8,128)(2,1)} %param.19) | data formatting | bytes 98304 | tf_op args[7]
  3.5 1.3 %copy.31 = bf16[16,16,3,256]{3,2,1,0:T(4,128)(2,1)S(1)} copy(bf16[16,16,3,256]{3,1,2,0:T(8,128)(2,1)} %param.21) | data formatting | bytes 786432 | tf_op args[9]
  4.9 0.7 select_convert_fusion.labels
  5.6 2.0 %shard_map.131 = (bf16[512,256]{1,0:T(8,128)(2,1)}, bf16[32,896]{1,0:T(8,128)(2,1)}) custom-call(f32[4]{0:T(128)} %weights.1, bf16[4,512,256]{2,1,0:T(8,128)(2,1)} %streams.3, bf16[32,3,256]{2,1,0:T(4,128)(2,1)} %copy.30.qkv, bf16[32,128]{1,0:T(8,128)(2,1)} %select_convert_fusion.labels), custom_call_target="tpu_custom_call" | custom-call | tf_op jit(solution)/shard_map/pallas_call | solution.py:272
  7.6 43.8 %shard_map.132 = (bf16[512,2048]{1,0:T(8,128)(2,1)}, bf16[4,8,2,32,896]{4,3,2,1,0:T(8,128)(2,1)}, bf16[4,8,2,32,256]{4,3,2,1,0:T(8,128)(2,1)}, bf16[8,2,16,2048]{3,2,1,0:T(8,128)(2,1)}) custom-call(bf16[512,256]{1,0:T(8,128)(2,1)} %get-tuple-element.8.mixed, bf16[32,896]{1,0:T(8,128)(2,1)} %get-tuple-element.9.rows, bf16[32,256]{1,0:T(8,128)(2,1)} %out_rows.1, ...), custom_call_target="tpu_custom_call" | custom-call | tf_op jit(solution)/shard_map/pallas_call | solution.py:234
  51.4 2.2 %fusion = f32[512]{0:T(512)S(1)} fusion(bf16[512,2048]{1,0:T(8,128)(2,1)} %get-tuple-element.10), kind=kLoop, calls=%fused_computation.2 | loop fusion | flops 3145216 | bytes 2099200 | tf_op jit(solution)/shard_map/reduce_sum | solution.py:424
  53.8 3.0 %fusion.2 = f32[512,512]{1,0:T(8,128)S(1)} fusion(bf16[2048,896]{1,0:T(8,128)(2,1)} %bitcast.22, bf16[512,2048]{1,0:T(8,128)(2,1)S(1)} %copy-done.1, f32[512]{0:T(512)S(1)} %add_rsqrt_fusion), kind=kOutput, calls=%fused_computation.4 | convolution fusion | flops 1076887552 | bytes 5244928 | tf_op jit(solution)/shard_map/dot_general | solution.py:447
  56.8 0.8 fusion.8
  57.5 1.1 fusion.6
  58.6 2.1 %shard_map.135 = bf16[128,16,512]{2,1,0:T(8,128)(2,1)} custom-call(s32[32]{0:T(128)} %multiply_add_fusion.placement, bf16[32,16,512]{2,1,0:T(8,128)(2,1)} %bitcast.17), custom_call_target="tpu_custom_call" | custom-call | tf_op jit(solution)/shard_map/pallas_call | solution.py:302
  60.8 9.3 %all-to-all-start = ((bf16[128,16,512]{2,1,0:T(8,128)(2,1)}), bf16[128,16,512]{2,1,0:T(8,128)(2,1)}, u32[]{:S(2)}, u32[]{:S(2)}) async-start(bf16[128,16,512]{2,1,0:T(8,128)(2,1)} %shard_map.135), calls=%async_computation | async-start | bytes 4194304 | tf_op jit(solution)/shard_map/all_to_all | solution.py:477
  70.1 1.1 slice.69
  71.1 0.2 copy.40
  71.4 0.2 fusion.22
  71.6 2.0 %fusion.7 = bf16[512,256]{1,0:T(8,128)(2,1)S(1)} fusion(f32[512,256]{1,0:T(8,128)S(1)} %fusion.22, bf16[2048,896]{1,0:T(8,128)(2,1)} %bitcast.24, bf16[512,2048]{1,0:T(8,128)(2,1)S(1)} %copy-done.1, f32[512]{0:T(512)S(1)} %add_rsqrt_fusion), kind=kOutput, calls=%fused_computation.14 | convolution fusion | flops 540278784 | bytes 3934208 | tf_op jit(solution)/shard_map/dot_general | solution.py:447
  73.7 0.4 fusion.35
  74.1 0.2 fusion.13
  74.3 0.4 fusion.36
  74.6 0.2 fusion.12
  74.8 0.4 convolution_convert_fusion
  75.2 0.4 convolution_convert_fusion.1
  75.6 0.7 pad_maximum_fusion.own
  76.3 24.7 %shard_map.133.attended = bf16[512,2048]{1,0:T(8,128)(2,1)} custom-call(bf16[512,256]{1,0:T(8,128)(2,1)} %pad_maximum_fusion.own), custom_call_target="tpu_custom_call" | custom-call | bytes 60000000 | tf_op jit(solution)/shard_map/pallas_call | solution.py:358
  101.1 3.1 %fusion.9.depth = f32[512,4]{1,0:T(8,128)} fusion(bf16[2048,4]{0,1:T(4,128)(2,1)S(1)} %copy-done, f32[4]{0:T(128)S(1)} %copy-done.6, bf16[512,2048]{1,0:T(8,128)(2,1)} %get-tuple-element.10, f32[512]{0:T(512)S(1)} %add_rsqrt_fusion), kind=kOutput, calls=%fused_computation.17 | convolution fusion | flops 11536384 | bytes 2123792 | tf_op jit(solution)/shard_map/dot_general | solution.py:472
  104.1 4.9 %shard_map.134 = bf16[4,512,256]{2,1,0:T(8,128)(2,1)} custom-call(f32[4,4]{1,0:T(4,128)} %mixing.1, bf16[512,2048]{1,0:T(8,128)(2,1)} %shard_map.133.attended, bf16[2048,256]{1,0:T(8,128)(2,1)} %bitcast.20, f32[512,4]{1,0:T(8,128)} %fusion.9.depth, bf16[4,512,256]{2,1,0:T(8,128)(2,1)} %streams.3), custom_call_target="tpu_custom_call" | custom-call | flops 600000000 | bytes 6000000 | tf_op jit(solution)/shard_map/pallas_call | solution.py:340
  109.1 0.7 select_reduce_fusion.chosen
  109.8 11.5 %all-to-all-done.incoming = bf16[128,16,512]{2,1,0:T(8,128)(2,1)} async-done(((bf16[128,16,512]{2,1,0:T(8,128)(2,1)}), bf16[128,16,512]{2,1,0:T(8,128)(2,1)}, u32[]{:S(2)}, u32[]{:S(2)}) %all-to-all-start) | async-done | bytes 2097184 | tf_op jit(solution)/shard_map/all_to_all | solution.py:477
  121.3 2.4 %shard_map.136 = bf16[32,16,512]{2,1,0:T(8,128)(2,1)} custom-call(s32[32]{0:T(128)} %select_reduce_fusion.chosen, bf16[128,16,512]{2,1,0:T(8,128)(2,1)} %all-to-all-done.incoming), custom_call_target="tpu_custom_call" | custom-call | tf_op jit(solution)/shard_map/pallas_call | solution.py:318
  123.7 2.0 %reshape.126 = bf16[32,16,2,256]{3,2,1,0:T(2,128)(2,1)} reshape(bf16[32,16,512]{2,1,0:T(8,128)(2,1)} %shard_map.136) | data formatting | bytes 1048576 | tf_op jit(solution)/shard_map/reshape | solution.py:478
  (24 shorter events, 0.3 us)
Async XLA Ops:
  0.6 100.4 %copy-start = (bf16[2048,4]{0,1:T(4,128)(2,1)S(1)}, bf16[2048,4]{0,1:T(4,128)(2,1)}, u32[]{:S(2)}) copy-start(bf16[2048,4]{0,1:T(4,128)(2,1)} %param.18) | copy-start | bytes 49156
  4.8 48.9 %copy-start.3 = (s32[1,512]{1,0:T(1,128)S(1)}, s32[1,512]{1,0:T(1,128)}, u32[]{:S(2)}) copy-start(s32[1,512]{1,0:T(1,128)} %param.13) | copy-start | bytes 6148
  4.8 48.9 %copy-start.4 = (s32[1,4,1]{1,2,0:T(1,128)S(1)}, s32[1,4,1]{1,2,0:T(1,128)}, u32[]{:S(2)}) copy-start(s32[1,4,1]{1,2,0:T(1,128)} %param.14) | copy-start | bytes 52
  51.4 2.4 %copy-start.1 = (bf16[512,2048]{1,0:T(8,128)(2,1)S(1)}, bf16[512,2048]{1,0:T(8,128)(2,1)}, u32[]{:S(2)}) copy-start(bf16[512,2048]{1,0:T(8,128)(2,1)} %get-tuple-element.10) | copy-start | bytes 6291460
  53.8 3.0 %copy-start.5 = (bf16[8,2,16,2048]{3,2,1,0:T(8,128)(2,1)S(1)}, bf16[8,2,16,2048]{3,2,1,0:T(8,128)(2,1)}, u32[]{:S(2)}) copy-start(bf16[8,2,16,2048]{3,2,1,0:T(8,128)(2,1)} %get-tuple-element.12) | copy-start | bytes 3145732
  60.8 60.5 %all-to-all-start = ((bf16[128,16,512]{2,1,0:T(8,128)(2,1)}), bf16[128,16,512]{2,1,0:T(8,128)(2,1)}, u32[]{:S(2)}, u32[]{:S(2)}) async-start(bf16[128,16,512]{2,1,0:T(8,128)(2,1)} %shard_map.135), calls=%async_computation | async-start | bytes 4194304 | tf_op jit(solution)/shard_map/all_to_all | solution.py:477
  71.6 2.1 %copy-start.2 = (bf16[512,512]{1,0:T(8,128)(2,1)S(1)}, bf16[512,512]{1,0:T(8,128)(2,1)}, u32[]{:S(2)}) copy-start(bf16[512,512]{1,0:T(8,128)(2,1)} %fusion.6) | copy-start | bytes 1572868
  75.6 25.5 %copy-start.6 = (f32[4]{0:T(128)S(1)}, f32[4]{0:T(128)}, u32[]{:S(2)}) copy-start(f32[4]{0:T(128)} %param.17) | copy-start | bytes 52

commit v5 on v3

--- a/solution.py
+++ b/solution.py
@@ -345,7 +345,9 @@
             pltpu.SemaphoreType.DMA((14,)),
             pltpu.SemaphoreType.DMA((2,)),
         ],
-        compiler_params=pltpu.CompilerParams(collective_id=1, has_side_effects=True),
+        compiler_params=pltpu.CompilerParams(
+            collective_id=1, has_side_effects=True, vmem_limit_bytes=66_000_000
+        ),
         cost_estimate=pl.CostEstimate(flops=0, bytes_accessed=60_000_000, transcendentals=0),
     )(own)
 

time: 126 us -> 126 us (level)
  local copies, waits for them, and re-layouts: 6.8 us -> 5.46 us
    unnamed x19 -> x17, local copies, waits for them, and re-layouts: 2.95 us -> 1.61 us
where the time goes in v5:
time: 126 us; the launch traced here: 125 us
  Pallas kernels  79.9 us (63%)
  matrix products  11.6 us (9%)
  waiting for transfers between devices  11.5 us (9%)
  starting transfers between devices  9.29 us (7%)
  other arithmetic  6.25 us (5%)
  local copies, waits for them, and re-layouts  5.46 us (4%)
    pallas_call x1, Pallas kernels, gather_all(): pl.pallas_call(gather_kernel, out_shape=[jax.ShapeDtypeStruct((tokens, wi...  43.8 us
    pallas_call x1, Pallas kernels, gather_tokens(): pl.pallas_call(tokens_kernel, out_shape=jax.ShapeDtypeStruct((tokens, wid...  24.7 us
    all_to_all x1, waiting for transfers between devices, body(): lax.all_to_all(outgoing, 'req', split_axis=0, concat_axis=0, tiled=True)  11.5 us
    all_to_all x1, starting transfers between devices, body(): lax.all_to_all(outgoing, 'req', split_axis=0, concat_axis=0, tiled=True)  9.29 us
    dot_general x2, matrix products, project(): jnp.dot(normed, qkv_all[:, start:stop], preferred_element_type=jnp.float32)  5 us
    pallas_call x1, Pallas kernels, finish(): pl.pallas_call(finish_kernel, grid=(tokens // block,), out_shape=jax.Shap...  4.89 us
    dot_general x1, matrix products, body(): jnp.dot(normed, depth_dir, preferred_element_type=jnp.float32)  3.05 us
  transfers between devices with their start and end apart: 1, of which 1 were waited for; matrix products, arithmetic and copies ran while one was open for 8% of the time, Pallas kernels for 24%

profile of v5, /device:TPU:1, one launch (start us, length us, event | category | flops | bytes accessed | tf_op | source)
XLA Modules:
  0.0 125.0 jit_solution(10910269800209300487)
XLA Ops:
  0.7 0.7 and_select_fusion.1
  1.3 0.2 convert_reduce_fusion
  1.5 0.5 multiply_add_fusion.placement
  2.0 0.8 copy.41
  2.8 1.3 %copy.31 = bf16[16,16,3,256]{3,2,1,0:T(4,128)(2,1)S(1)} copy(bf16[16,16,3,256]{3,1,2,0:T(8,128)(2,1)} %param.21) | data formatting | bytes 786432 | tf_op args[9]
  4.3 0.6 pad_maximum_fusion.1.rows
  4.9 2.0 %shard_map.131.mixed = bf16[512,256]{1,0:T(8,128)(2,1)} custom-call(f32[4]{0:T(128)} %weights.1, bf16[4,512,256]{2,1,0:T(8,128)(2,1)} %streams.3), custom_call_target="tpu_custom_call" | custom-call | tf_op jit(solution)/shard_map/pallas_call | solution.py:263
  6.9 43.8 %shard_map.132 = (bf16[512,2048]{1,0:T(8,128)(2,1)}, bf16[4,8,2,32,896]{4,3,2,1,0:T(8,128)(2,1)}, bf16[4,8,2,32,256]{4,3,2,1,0:T(8,128)(2,1)}, bf16[8,2,16,2048]{3,2,1,0:T(8,128)(2,1)}) custom-call(bf16[512,256]{1,0:T(8,128)(2,1)} %shard_map.131.mixed, bf16[32,896]{1,0:T(8,128)(2,1)} %pad_maximum_fusion.1.rows, bf16[32,256]{1,0:T(8,128)(2,1)} %out_rows.1, ...), custom_call_target="tpu_custom_call" | custom-call | tf_op jit(solution)/shard_map/pallas_call | solution.py:234
  50.7 2.2 %fusion = f32[512]{0:T(512)S(1)} fusion(bf16[512,2048]{1,0:T(8,128)(2,1)} %get-tuple-element.6), kind=kLoop, calls=%fused_computation.2 | loop fusion | flops 3145216 | bytes 2099200 | tf_op jit(solution)/shard_map/reduce_sum | solution.py:404
  53.1 3.0 %fusion.2 = f32[512,512]{1,0:T(8,128)S(1)} fusion(bf16[2048,896]{1,0:T(8,128)(2,1)} %bitcast.25, bf16[512,2048]{1,0:T(8,128)(2,1)S(1)} %copy-done.1, f32[512]{0:T(512)S(1)} %add_rsqrt_fusion), kind=kOutput, calls=%fused_computation.4 | convolution fusion | flops 1076887552 | bytes 5244928 | tf_op jit(solution)/shard_map/dot_general | solution.py:427
  56.1 0.8 fusion.8
  56.8 1.1 fusion.6
  57.9 2.1 %shard_map.135 = bf16[128,16,512]{2,1,0:T(8,128)(2,1)} custom-call(s32[32]{0:T(128)} %multiply_add_fusion.placement, bf16[32,16,512]{2,1,0:T(8,128)(2,1)} %bitcast.19), custom_call_target="tpu_custom_call" | custom-call | tf_op jit(solution)/shard_map/pallas_call | solution.py:282
  60.1 9.3 %all-to-all-start = ((bf16[128,16,512]{2,1,0:T(8,128)(2,1)}), bf16[128,16,512]{2,1,0:T(8,128)(2,1)}, u32[]{:S(2)}, u32[]{:S(2)}) async-start(bf16[128,16,512]{2,1,0:T(8,128)(2,1)} %shard_map.135), calls=%async_computation | async-start | bytes 4194304 | tf_op jit(solution)/shard_map/all_to_all | solution.py:457
  69.4 1.1 slice.69
  70.5 0.2 copy.40
  70.7 0.2 fusion.22
  70.9 2.0 %fusion.7 = bf16[512,256]{1,0:T(8,128)(2,1)S(1)} fusion(f32[512,256]{1,0:T(8,128)S(1)} %fusion.22, bf16[2048,896]{1,0:T(8,128)(2,1)} %bitcast.27, bf16[512,2048]{1,0:T(8,128)(2,1)S(1)} %copy-done.1, f32[512]{0:T(512)S(1)} %add_rsqrt_fusion), kind=kOutput, calls=%fused_computation.14 | convolution fusion | flops 540278784 | bytes 3934208 | tf_op jit(solution)/shard_map/dot_general | solution.py:427
  73.0 0.4 fusion.35
  73.4 0.2 fusion.13
  73.6 0.4 fusion.36
  73.9 0.2 fusion.12
  74.1 0.4 convolution_convert_fusion
  74.5 0.4 convolution_convert_fusion.1
  74.9 0.7 pad_maximum_fusion.own
  75.7 24.7 %shard_map.133.attended = bf16[512,2048]{1,0:T(8,128)(2,1)} custom-call(bf16[512,256]{1,0:T(8,128)(2,1)} %pad_maximum_fusion.own), custom_call_target="tpu_custom_call" | custom-call | bytes 60000000 | tf_op jit(solution)/shard_map/pallas_call | solution.py:338
  100.4 3.1 %fusion.9.depth = f32[512,4]{1,0:T(8,128)} fusion(bf16[2048,4]{0,1:T(4,128)(2,1)S(1)} %copy-done, f32[4]{0:T(128)S(1)} %copy-done.6, bf16[512,2048]{1,0:T(8,128)(2,1)} %get-tuple-element.6, f32[512]{0:T(512)S(1)} %add_rsqrt_fusion), kind=kOutput, calls=%fused_computation.17 | convolution fusion | flops 11536384 | bytes 2123792 | tf_op jit(solution)/shard_map/dot_general | solution.py:452
  103.4 4.9 %shard_map.134 = bf16[4,512,256]{2,1,0:T(8,128)(2,1)} custom-call(f32[4,4]{1,0:T(4,128)} %mixing.1, bf16[512,2048]{1,0:T(8,128)(2,1)} %shard_map.133.attended, bf16[2048,256]{1,0:T(8,128)(2,1)} %bitcast.22, f32[512,4]{1,0:T(8,128)} %fusion.9.depth, bf16[4,512,256]{2,1,0:T(8,128)(2,1)} %streams.3), custom_call_target="tpu_custom_call" | custom-call | flops 600000000 | bytes 6000000 | tf_op jit(solution)/shard_map/pallas_call | solution.py:320
  108.4 0.7 select_reduce_fusion.chosen
  109.1 11.5 %all-to-all-done.incoming = bf16[128,16,512]{2,1,0:T(8,128)(2,1)} async-done(((bf16[128,16,512]{2,1,0:T(8,128)(2,1)}), bf16[128,16,512]{2,1,0:T(8,128)(2,1)}, u32[]{:S(2)}, u32[]{:S(2)}) %all-to-all-start) | async-done | bytes 2097184 | tf_op jit(solution)/shard_map/all_to_all | solution.py:457
  120.6 2.4 %shard_map.136 = bf16[32,16,512]{2,1,0:T(8,128)(2,1)} custom-call(s32[32]{0:T(128)} %select_reduce_fusion.chosen, bf16[128,16,512]{2,1,0:T(8,128)(2,1)} %all-to-all-done.incoming), custom_call_target="tpu_custom_call" | custom-call | tf_op jit(solution)/shard_map/pallas_call | solution.py:298
  123.0 2.0 %reshape.130 = bf16[32,16,2,256]{3,2,1,0:T(2,128)(2,1)} reshape(bf16[32,16,512]{2,1,0:T(8,128)(2,1)} %shard_map.136) | data formatting | bytes 1048576 | tf_op jit(solution)/shard_map/reshape | solution.py:458
  (25 shorter events, 0.4 us)
Async XLA Ops:
  0.6 99.7 %copy-start = (bf16[2048,4]{0,1:T(4,128)(2,1)S(1)}, bf16[2048,4]{0,1:T(4,128)(2,1)}, u32[]{:S(2)}) copy-start(bf16[2048,4]{0,1:T(4,128)(2,1)} %param.18) | copy-start | bytes 49156
  4.2 48.8 %copy-start.3 = (s32[1,512]{1,0:T(1,128)S(1)}, s32[1,512]{1,0:T(1,128)}, u32[]{:S(2)}) copy-start(s32[1,512]{1,0:T(1,128)} %param.13) | copy-start | bytes 6148
  4.2 48.8 %copy-start.4 = (s32[1,4,1]{1,2,0:T(1,128)S(1)}, s32[1,4,1]{1,2,0:T(1,128)}, u32[]{:S(2)}) copy-start(s32[1,4,1]{1,2,0:T(1,128)} %param.14) | copy-start | bytes 52
  50.7 2.4 %copy-start.1 = (bf16[512,2048]{1,0:T(8,128)(2,1)S(1)}, bf16[512,2048]{1,0:T(8,128)(2,1)}, u32[]{:S(2)}) copy-start(bf16[512,2048]{1,0:T(8,128)(2,1)} %get-tuple-element.6) | copy-start | bytes 6291460
  53.1 3.0 %copy-start.5 = (bf16[8,2,16,2048]{3,2,1,0:T(8,128)(2,1)S(1)}, bf16[8,2,16,2048]{3,2,1,0:T(8,128)(2,1)}, u32[]{:S(2)}) copy-start(bf16[8,2,16,2048]{3,2,1,0:T(8,128)(2,1)} %get-tuple-element.8) | copy-start | bytes 3145732
  60.1 60.5 %all-to-all-start = ((bf16[128,16,512]{2,1,0:T(8,128)(2,1)}), bf16[128,16,512]{2,1,0:T(8,128)(2,1)}, u32[]{:S(2)}, u32[]{:S(2)}) async-start(bf16[128,16,512]{2,1,0:T(8,128)(2,1)} %shard_map.135), calls=%async_computation | async-start | bytes 4194304 | tf_op jit(solution)/shard_map/all_to_all | solution.py:457
  70.9 2.1 %copy-start.2 = (bf16[512,512]{1,0:T(8,128)(2,1)S(1)}, bf16[512,512]{1,0:T(8,128)(2,1)}, u32[]{:S(2)}) copy-start(bf16[512,512]{1,0:T(8,128)(2,1)} %fusion.6) | copy-start | bytes 1572868
  74.9 25.5 %copy-start.6 = (f32[4]{0:T(128)S(1)}, f32[4]{0:T(128)}, u32[]{:S(2)}) copy-start(f32[4]{0:T(128)} %param.17) | copy-start | bytes 52
